TPU v7x, 32 devices: a whole 2x2x4 slice. The times are simulated.
32 devices in a mesh: fsdp: 8 (over z, x), side: 4 (over y, core).
Axes of the slice: x: 2, y: 2, z: 4, core: 2. Of those that a mesh axis runs over, the one named last changes fastest.
Arguments:
- attn_inputs: bfloat16 [4096, 5120], P(('side', 'fsdp')), may hold values from -6 to 6
- queries: bfloat16 [4096, 2560], P(('side', 'fsdp')), may hold values from -310 to 310
- key_vectors: bfloat16 [4096, 512], P(('side', 'fsdp')), may hold values from -12 to 12
- logp_grad: bfloat16 [4096, 2560], P(('side', 'fsdp')), may hold values from -24 to 24
- new_logp: float32 [4096], P(('side', 'fsdp')), may hold values from -6.5 to -0.01
- old_logp: float32 [4096], P(('side', 'fsdp')), may hold values from -4 to -0.05
- rewards: float32 [8], replicated, may hold values from -8 to 8
- group_ids: int32 [8], replicated, may hold values from 0 to 1
- lengths: int32 [8], replicated, may hold values from 256 to 512
- value_proj: bfloat16 [5120, 512], P('fsdp'), may hold values from -0.078125 to 0.078125
- first_moment: bfloat16 [5120, 512], P(('fsdp', 'side')), may hold values from -120 to 120
- second_moment: bfloat16 [5120, 512], P(('fsdp', 'side')), may hold values from 100 to 9984
Outputs:
- input_grad: bfloat16 [4096, 5120], P(('side', 'fsdp'))
- new_proj: bfloat16 [5120, 512], P('fsdp')
- new_first: bfloat16 [5120, 512], P(('fsdp', 'side'))
- new_second: bfloat16 [5120, 512], P(('fsdp', 'side'))
All inputs are finite; a program needn't handle non-finite values.
Results may differ from a plain program's by a relative error of at most 0.03.
Values may be sent and summed in bfloat16 or wider, within the bound.
No kernel may reach another device: no remote copies, remote signals or barrier semaphores. Data moves between devices by JAX's collectives and lax.ppermute only.
A program may use at most 64 MiB of HBM per device.

v0:
```python
import functools
import math

import jax
import jax.numpy as jnp
from jax import lax
from jax.experimental import pallas as pl
from jax.experimental.pallas import tpu as pltpu
from jax.sharding import Mesh
from jax.sharding import PartitionSpec as P


HEAD = 128
ROLLS = 2
PAIR = 2


clip_low = 0.8
clip_high = 1.2
decay_first = 0.9
decay_second = 0.95
step_rate = 0.001
weight_decay = 0.1
adam_eps = 1e-08
bias_first = 1.0 - 0.9**10
bias_second = 1.0 - 0.95**10

ROOM = pltpu.CompilerParams(vmem_limit_bytes=16 * 2**20)


def coefficient_kernel(full_len, place, rewards, group_ids, lengths, new_lp, old_lp, out):
    count_all = rewards.shape[0]
    shape = out.shape
    half = shape[1] // ROLLS
    lane = lax.broadcasted_iota(jnp.int32, shape, 1)
    adv_tok = jnp.zeros(shape, jnp.float32)
    len_tok = jnp.zeros(shape, jnp.int32)
    pos_tok = lane + (place[0] * PAIR + place[1]) * half
    for roll in range(ROLLS):
        mine = (place[2] * 2 + place[3]) * ROLLS + roll
        same = [group_ids[n] == group_ids[mine] for n in range(count_all)]
        values = [jnp.full(shape, rewards[n], jnp.float32) for n in range(count_all)]
        count = sum(jnp.full(shape, jnp.where(flag, 1.0, 0.0), jnp.float32) for flag in same)
        mean = sum(jnp.where(flag, value, 0.0) for flag, value in zip(same, values)) / count
        variance = (
            sum(
                jnp.where(flag, (value - mean) * (value - mean), 0.0)
                for flag, value in zip(same, values)
            )
            / count
        )
        spread = jnp.full(shape, rewards[mine], jnp.float32) - mean
        advantage = spread / jnp.maximum(jnp.sqrt(variance), 1.0)
        here = (lane >= roll * half) & (lane < (roll + 1) * half)
        adv_tok = jnp.where(here, advantage, adv_tok)
        len_tok = jnp.where(here, lengths[mine], len_tok)
        pos_tok = jnp.where(here, pos_tok - roll * half, pos_tok)
    ratio_now = jnp.exp(new_lp[...] - old_lp[...])
    clipped = jnp.clip(ratio_now, clip_low, clip_high)
    active = (ratio_now * adv_tok <= clipped * adv_tok) & (pos_tok < len_tok)
    len_weight = full_len / len_tok.astype(jnp.float32)
    out[...] = jnp.where(active, -adv_tok * ratio_now * len_weight, 0.0)


def coefficients(place, rewards, group_ids, lengths, new_logp, old_logp, full_len):
    shape = (1, new_logp.shape[0])
    scalars = pl.BlockSpec(memory_space=pltpu.SMEM)
    whole = pl.BlockSpec(memory_space=pltpu.VMEM)
    return pl.pallas_call(
        functools.partial(coefficient_kernel, full_len),
        in_specs=[scalars] * 4 + [whole] * 2,
        out_specs=whole,
        out_shape=jax.ShapeDtypeStruct(shape, jnp.float32),
        compiler_params=ROOM,
    )(place, rewards, group_ids, lengths, new_logp.reshape(shape), old_logp.reshape(shape))


def attention_kernel(slots, half, place, q_own, q_far, g_own, g_far, c_own, c_far, *refs):
    key_refs, part_refs, probs = refs[:slots], refs[slots : 2 * slots], refs[2 * slots]
    z_index, x_index = place[0], place[1]
    per_group = q_own.shape[1] // HEAD
    block = PAIR * half
    scale = math.log2(math.e) / math.sqrt(HEAD)

    def spot(dim):
        at = lax.broadcasted_iota(jnp.int32, (block, block), dim)
        return jnp.where(at < half, at + x_index * half, at - half + (1 - x_index) * half)

    causal = spot(0) <= spot(1)
    for roll in range(ROLLS):
        rows = slice(roll * half, (roll + 1) * half)
        far_rows = slice((ROLLS + roll) * half, (ROLLS + roll + 1) * half)
        keys = jnp.concatenate(
            [key_refs[n][part, :] for n in range(slots) for part in (rows, far_rows)], axis=0
        )
        grads = []
        coeff = jnp.concatenate([c_own[:, rows], c_far[:, rows]], axis=1)
        for head in range(per_group):
            cols = slice(head * HEAD, (head + 1) * HEAD)
            query = jnp.concatenate([q_own[rows, cols], q_far[rows, cols]], axis=0)
            grads += [g_own[rows, cols], g_far[rows, cols]]
            scores = (
                lax.dot_general(
                    keys, query, (((1,), (1,)), ((), ())), preferred_element_type=jnp.float32
                )
                * scale
            )
            pieces = [jnp.where(causal, scores[:block], -1e30)]
            for n in range(1, slots):
                pieces.append(
                    jnp.where(z_index >= n, scores[n * block : (n + 1) * block], -1e30)
                )
            top = functools.reduce(
                jnp.maximum, [jnp.max(piece, axis=0, keepdims=True) for piece in pieces]
            )
            expo = [jnp.exp2(piece - top) for piece in pieces]
            total = sum(jnp.sum(piece, axis=0, keepdims=True) for piece in expo)
            weight = coeff / total
            for n in range(slots):
                probs[n * block : (n + 1) * block, head * block : (head + 1) * block] = (
                    expo[n] * weight
                ).astype(jnp.bfloat16)
        summed = jnp.dot(
            probs[...], jnp.concatenate(grads, axis=0), preferred_element_type=jnp.float32
        ).astype(jnp.bfloat16)
        for n in range(slots):
            part_refs[n][rows, :] = summed[n * block : n * block + half]
            part_refs[n][far_rows, :] = summed[n * block + half : (n + 1) * block]


def attention_parts(place, queries, q_far, logp_grad, g_far, c_own, c_far, key_blocks):
    slots = len(key_blocks)
    tok_rows, q_cols = q_far.shape
    kv_heads = key_blocks[0].shape[1] // HEAD
    per_head = q_cols // kv_heads
    half = tok_rows // ROLLS
    own_spec = pl.BlockSpec((tok_rows, per_head), lambda h, place: (0, place[1] * kv_heads + h))
    far_spec = pl.BlockSpec((tok_rows, per_head), lambda h, place: (0, h))
    coeff_spec = pl.BlockSpec(c_own.shape, lambda h, place: (0, 0))
    k_spec = pl.BlockSpec((PAIR * tok_rows, HEAD), lambda h, place: (0, h))
    shape = jax.ShapeDtypeStruct(key_blocks[0].shape, jnp.bfloat16)
    work = 4 * kv_heads * per_head * ROLLS * (PAIR * half) ** 2 * slots
    return pl.pallas_call(
        functools.partial(attention_kernel, slots, half),
        grid_spec=pltpu.PrefetchScalarGridSpec(
            num_scalar_prefetch=1,
            grid=(kv_heads,),
            in_specs=[own_spec, far_spec] * 2 + [coeff_spec] * 2 + [k_spec] * slots,
            out_specs=[k_spec] * slots,
            scratch_shapes=[
                pltpu.VMEM(
                    (slots * PAIR * half, per_head // HEAD * PAIR * half), jnp.bfloat16
                )
            ],
        ),
        out_shape=[shape] * slots,
        compiler_params=ROOM,
        cost_estimate=pl.CostEstimate(
            flops=work, bytes_accessed=8 * tok_rows * q_cols, transcendentals=work // 256
        ),
    )(place, queries, q_far, logp_grad, g_far, c_own, c_far, *key_blocks)


def pack_kernel(tok_rows, keys, queries, grads, key_room, k_far, q_far, g_far, sems):
    x_index = lax.axis_index("x")

    def half(array, index):
        cols = array.shape[1] // PAIR
        return array.at[:, pl.ds(pl.multiple_of(index * cols, HEAD), cols)]

    copies = [
        pltpu.make_async_copy(source, target, sems.at[n])
        for n, (source, target) in enumerate(
            [
                (half(keys, 1 - x_index), k_far),
                (half(keys, x_index), key_room.at[pl.ds(0, tok_rows), :]),
                (half(queries, 1 - x_index), q_far),
                (half(grads, 1 - x_index), g_far),
            ]
        )
    ]
    for copy in copies:
        copy.start()
    for copy in copies:
        copy.wait()


def packed(key_vectors, queries, logp_grad):
    tok_rows = queries.shape[0]

    def half(array, rows):
        return jax.ShapeDtypeStruct((rows, array.shape[1] // PAIR), jnp.bfloat16)

    return pl.pallas_call(
        functools.partial(pack_kernel, tok_rows),
        in_specs=[pl.BlockSpec(memory_space=pl.ANY)] * 3,
        out_specs=[pl.BlockSpec(memory_space=pltpu.VMEM)] * 4,
        out_shape=[
            half(key_vectors, PAIR * tok_rows),
            half(key_vectors, tok_rows),
            half(queries, tok_rows),
            half(logp_grad, tok_rows),
        ],
        scratch_shapes=[pltpu.SemaphoreType.DMA((4,))],
        cost_estimate=pl.CostEstimate(
            flops=0, bytes_accessed=4 * queries.size, transcendentals=0
        ),
    )(key_vectors, queries, logp_grad)


def owner_kernel(pieces, z_size, place, near, far, *refs):
    values, outs = refs[: 2 * pieces], refs[2 * pieces : 2 * pieces + z_size]
    token_rows = refs[2 * pieces + z_size]
    buffers, totals, sems = refs[-3:]
    copies = [
        pltpu.make_async_copy(source, buffers.at[n], sems.at[n])
        for n, source in enumerate((near, far))
    ]
    for copy in copies:
        copy.start()
    sides = near.shape[0] // PAIR
    rows, tokens = near.shape[2:]
    half = values[0].shape[1]
    for n, copy in enumerate(copies):
        copy.wait()
        for m in range(PAIR):
            columns = jnp.concatenate(
                [
                    buffers[n, (x + m) % PAIR * sides + y].reshape(z_size * rows, tokens)
                    for y in range(sides)
                    for x in range(PAIR)
                ],
                axis=1,
            )
            blocks = values[m * pieces + n * sides : m * pieces + (n + 1) * sides]
            product = jnp.dot(
                columns,
                jnp.concatenate([ref[...] for ref in blocks], axis=0),
                preferred_element_type=jnp.float32,
            )
            part = slice(m * half, (m + 1) * half)
            totals[:, part] = product if n == 0 else totals[:, part] + product
    flag = place[1] == 0
    for x in range(PAIR):
        for y in range(sides):
            low = values[y][x * tokens : (x + 1) * tokens, :]
            high = values[pieces + y][(1 - x) * tokens : (2 - x) * tokens, :]
            at = (x * sides + y) * tokens
            token_rows[at : at + tokens, :half] = jnp.where(flag, low, high)
            token_rows[at : at + tokens, half:] = jnp.where(flag, high, low)
    for k, out in enumerate(outs):
        at = place[0] + k
        start = pl.multiple_of(jnp.where(at >= z_size, at - z_size, at) * rows, rows)
        out[...] = totals[pl.ds(start, rows), :].astype(jnp.bfloat16)


def plain_owner_products(place, near, far, first, second):
    z_size, rows, tokens = near.shape[1:]
    sides = near.shape[0] // PAIR
    halves = []
    for m, blocks in enumerate((first, second)):
        total = 0.0
        for n, array in enumerate((near, far)):
            order = [(x + m) % PAIR * sides + y for y in range(sides) for x in range(PAIR)]
            columns = jnp.stack([array[at] for at in order], axis=2)
            total = total + jnp.dot(
                columns.reshape(z_size * rows, -1),
                jnp.concatenate(blocks[n * sides : (n + 1) * sides], axis=0),
                preferred_element_type=jnp.float32,
            )
        halves.append(total.astype(jnp.bfloat16))
    every = jnp.concatenate(halves, axis=1).reshape(z_size, rows, -1)
    groups = []
    for x in range(PAIR):
        for y in range(sides):
            low = first[y][x * tokens : (x + 1) * tokens]
            high = second[y][(1 - x) * tokens : (2 - x) * tokens]
            groups.append(
                jnp.where(
                    place[1] == 0,
                    jnp.concatenate([low, high], axis=1),
                    jnp.concatenate([high, low], axis=1),
                )
            )
    return [cut(every, turned(place[0], k, z_size), 0) for k in range(z_size)] + [
        jnp.concatenate(groups, axis=0)
    ]


def owner_products(place, near, far, first, second):
    z_size, rows, tokens = near.shape[1:]
    if rows % 16:
        return plain_owner_products(place, near, far, first, second)
    pieces = len(first)
    width = 2 * first[0].shape[1]
    whole = pl.BlockSpec(memory_space=pltpu.VMEM)
    shape = jax.ShapeDtypeStruct((rows, width), jnp.bfloat16)
    return pl.pallas_call(
        functools.partial(owner_kernel, pieces, z_size),
        in_specs=[pl.BlockSpec(memory_space=pltpu.SMEM)]
        + [pl.BlockSpec(memory_space=pl.ANY)] * 2
        + [whole] * (2 * pieces),
        out_specs=[whole] * (z_size + 1),
        out_shape=[shape] * z_size
        + [jax.ShapeDtypeStruct((near.shape[0] * tokens, width), jnp.bfloat16)],
        scratch_shapes=[
            pltpu.VMEM((2, *near.shape), jnp.bfloat16),
            pltpu.VMEM((z_size * rows, width), jnp.float32),
            pltpu.SemaphoreType.DMA((2,)),
        ],
        compiler_params=ROOM,
        cost_estimate=pl.CostEstimate(
            flops=4 * near.size * width, bytes_accessed=8 * near.size, transcendentals=0
        ),
    )(place, near, far, *first, *second)


def row_kernel(z_size, groups, place, token_rows, *refs):
    proj, outs = refs[:4], refs[4 : 4 + groups]
    rows_all, sems = refs[-2:]
    rows, tok_rows = proj[0].shape[1], outs[0].shape[0]
    copies = []
    for k, bits in enumerate(flips(z_size)):
        for c in range(2):
            at_core = place[3] if c == 0 else 1 - place[3]
            start = ((place[0] ^ bits) * 2 + at_core) * rows
            group, at = divmod(k, z_size // 2)
            copies.append(
                pltpu.make_async_copy(
                    proj[2 * c + group].at[at],
                    rows_all.at[pl.ds(pl.multiple_of(start, rows), rows), :],
                    sems.at[2 * k + c],
                )
            )
    for copy in copies:
        copy.start()
    for copy in copies:
        copy.wait()
    product = lax.dot_general(
        token_rows[...],
        rows_all[...],
        (((1,), (1,)), ((), ())),
        preferred_element_type=jnp.float32,
    ).astype(jnp.bfloat16)
    for n, out in enumerate(outs):
        out[...] = product[n * tok_rows : (n + 1) * tok_rows]


def plane_kernel(place, columns, *outs):
    y_size = columns.shape[2]
    for x in range(PAIR):
        for y in range(y_size):
            at_x, at_y = place[1] + x, place[2] + y
            at_x = jnp.where(at_x >= PAIR, at_x - PAIR, at_x)
            at_y = jnp.where(at_y >= y_size, at_y - y_size, at_y)
            out = outs[x * y_size + y]
            for z in range(columns.shape[0]):
                out[z] = columns[z, at_x, at_y]


def core_kernel(place, *refs):
    pieces, (near, far) = refs[:-2], refs[-2:]
    for n, piece in enumerate(pieces):
        for z in range(piece.shape[0]):
            near[n, z] = piece[z, place[3]]
            far[n, z] = piece[z, 1 - place[3]]


def sliced(kernel, place, arrays, shapes):
    whole = pl.BlockSpec(memory_space=pltpu.VMEM)
    return pl.pallas_call(
        kernel,
        in_specs=[pl.BlockSpec(memory_space=pltpu.SMEM)] + [whole] * len(arrays),
        out_specs=[whole] * len(shapes),
        out_shape=[jax.ShapeDtypeStruct(shape, jnp.bfloat16) for shape in shapes],
        compiler_params=ROOM,
        cost_estimate=pl.CostEstimate(
            flops=0,
            bytes_accessed=4 * sum(math.prod(shape) for shape in shapes),
            transcendentals=0,
        ),
    )(place, *arrays)


def by_place(blocks, index):
    size = len(blocks)
    back = jnp.stack([blocks[-k % size] for k in range(size)])
    start = jnp.where(index == 0, 0, size - index)
    return lax.dynamic_slice_in_dim(jnp.concatenate([back, back], axis=0), start, size, 0)


def plain_row_products(place, token_rows, groups, proj):
    width = proj[0].shape[2]
    z_size = 2 * proj[0].shape[0]
    cores = by_place(
        [jnp.concatenate(proj[2 * c : 2 * c + 2], axis=0) for c in range(2)], place[3]
    )
    order = {bits: k for k, bits in enumerate(flips(z_size))}
    along = jnp.stack([cores[:, order[k]] for k in range(z_size)])
    along = jnp.take(along, jnp.arange(z_size, dtype=jnp.int32) ^ place[0], axis=0)
    every = along.reshape(-1, width)
    product = jnp.dot(token_rows, every.T, preferred_element_type=jnp.float32)
    return jnp.split(product.astype(jnp.bfloat16), groups)


def row_products(place, token_rows, groups, proj):
    _, rows, width = proj[0].shape
    z_size = 2 * proj[0].shape[0]
    tok_rows = token_rows.shape[0] // groups
    cols = 2 * z_size * rows
    if rows % 16 or cols % 128:
        return plain_row_products(place, token_rows, groups, proj)
    whole = pl.BlockSpec(memory_space=pltpu.VMEM)
    shape = jax.ShapeDtypeStruct((tok_rows, cols), jnp.bfloat16)
    return pl.pallas_call(
        functools.partial(row_kernel, z_size, groups),
        in_specs=[pl.BlockSpec(memory_space=pltpu.SMEM), whole]
        + [pl.BlockSpec(memory_space=pl.ANY)] * len(proj),
        out_specs=[whole] * groups,
        out_shape=[shape] * groups,
        scratch_shapes=[
            pltpu.VMEM((cols, width), jnp.bfloat16),
            pltpu.SemaphoreType.DMA((2 * z_size,)),
        ],
        compiler_params=ROOM,
        cost_estimate=pl.CostEstimate(
            flops=2 * groups * tok_rows * width * cols,
            bytes_accessed=2 * cols * (width + groups * tok_rows),
            transcendentals=0,
        ),
    )(place, token_rows, *proj)


def final_kernel(z_size, place, *refs):
    pieces, out = refs[:-1], refs[-1]
    cols = pieces[0].shape[1] // z_size
    flags = place[1] == 0, place[2] == 0
    for z in range(z_size):
        part = slice(z * cols, (z + 1) * cols)
        near = [jnp.where(flags[1], pieces[y][:, part], pieces[1 - y][:, part]) for y in (0, 1)]
        far = [
            jnp.where(flags[1], pieces[2 + y][:, part], pieces[3 - y][:, part]) for y in (0, 1)
        ]
        near, far = jnp.concatenate(near, axis=1), jnp.concatenate(far, axis=1)
        wide = 2 * cols
        out[:, 2 * z * wide : (2 * z + 1) * wide] = jnp.where(flags[0], near, far)
        out[:, (2 * z + 1) * wide : (2 * z + 2) * wide] = jnp.where(flags[0], far, near)


def assembled(place, pieces, z_size):
    tokens = pieces[0].shape[0]
    y_size = len(pieces) // PAIR
    cols = pieces[0].shape[1] // z_size
    if y_size != 2 or 2 * cols % 128:
        split = [piece.reshape(tokens, z_size, cols) for piece in pieces]
        both = []
        for x in range(PAIR):
            found = jnp.stack(split[x * y_size : (x + 1) * y_size])
            start = jnp.where(place[2] == 0, 0, y_size - place[2])
            both.append(
                lax.dynamic_slice_in_dim(
                    jnp.concatenate([found, found], axis=0), start, y_size, 0
                )
            )
        both = jnp.stack(both)
        both = jnp.where(place[1] == 0, both, both[::-1])
        return both.transpose(2, 3, 0, 1, 4).reshape(tokens, -1)
    steps = 2 if tokens % 64 == 0 else 1

    def rows(array_cols):
        return pl.BlockSpec((tokens // steps, array_cols), lambda i, place: (i, 0))

    return pl.pallas_call(
        functools.partial(final_kernel, z_size),
        grid_spec=pltpu.PrefetchScalarGridSpec(
            num_scalar_prefetch=1,
            grid=(steps,),
            in_specs=[rows(z_size * cols)] * len(pieces),
            out_specs=rows(len(pieces) * z_size * cols),
        ),
        out_shape=jax.ShapeDtypeStruct((tokens, len(pieces) * z_size * cols), jnp.bfloat16),
        compiler_params=ROOM,
        cost_estimate=pl.CostEstimate(
            flops=0, bytes_accessed=4 * tokens * len(pieces) * z_size * cols, transcendentals=0
        ),
    )(place, *pieces)


def adam_rows(old_rows, grad_rows, first_moment, second_moment):
    first = decay_first * first_moment.astype(jnp.float32) + (1.0 - decay_first) * grad_rows
    second = (
        decay_second * second_moment.astype(jnp.float32)
        + (1.0 - decay_second) * grad_rows * grad_rows
    )
    weight_now = old_rows.astype(jnp.float32)
    update = (
        first / bias_first / (jnp.sqrt(second / bias_second) + adam_eps) + weight_decay * weight_now
    )
    return (
        (weight_now - step_rate * update).astype(jnp.bfloat16),
        first.astype(jnp.bfloat16),
        second.astype(jnp.bfloat16),
    )


def adam_kernel(place, count, *refs):
    pieces, (old_rows, first_moment, second_moment), outs = refs[:count], refs[count:-3], refs[-3:]
    grad = pieces[0][...].astype(jnp.float32)
    for piece in pieces[1:]:
        grad = grad + piece[...].astype(jnp.float32)
    mid = grad.shape[1] // 2
    swap = jnp.concatenate([grad[:, mid:], grad[:, :mid]], axis=1)
    grad = jnp.where(place[1] == 0, grad, swap)
    for out, value in zip(
        outs, adam_rows(old_rows[...], grad, first_moment[...], second_moment[...])
    ):
        out[...] = value


def adam_step(place, pieces, old_rows, first_moment, second_moment):
    arrays = [*pieces, old_rows, first_moment, second_moment]
    whole = pl.BlockSpec(memory_space=pltpu.VMEM)
    return pl.pallas_call(
        lambda place, *refs: adam_kernel(place, len(pieces), *refs),
        in_specs=[pl.BlockSpec(memory_space=pltpu.SMEM)] + [whole] * len(arrays),
        out_specs=[whole] * 3,
        out_shape=[jax.ShapeDtypeStruct(old_rows.shape, jnp.bfloat16)] * 3,
        compiler_params=ROOM,
        cost_estimate=pl.CostEstimate(
            flops=40 * old_rows.size,
            bytes_accessed=2 * (len(arrays) + 3) * old_rows.size,
            transcendentals=old_rows.size,
        ),
    )(place, *arrays)


def shift(value, axis, step, wrap=True):
    size = lax.axis_size(axis)
    pairs = [(i, (i + step) % size) for i in range(size) if wrap or 0 <= i + step < size]
    return lax.ppermute(value, axis, pairs)


def turned(index, step, size):
    moved = index + step
    return jnp.where(moved >= size, moved - size, moved)


def z_bits(z_size):
    assert z_size & (z_size - 1) == 0
    return [1 << n for n in range(z_size.bit_length() - 2, -1, -1)]


def flips(z_size):
    bits = z_bits(z_size)
    return [
        functools.reduce(int.__xor__, [bit for n, bit in enumerate(bits) if k >> n & 1], 0)
        for k in range(z_size)
    ]


def cut(value, index, dim):
    return lax.dynamic_index_in_dim(value, index, dim, keepdims=False)


def step(
    attn_inputs,
    queries,
    key_vectors,
    logp_grad,
    new_logp,
    old_logp,
    rewards,
    group_ids,
    lengths,
    value_proj,
    first_moment,
    second_moment,
):
    z_size, y_size, core_size = lax.axis_size("z"), lax.axis_size("y"), lax.axis_size("core")
    z_index, x_index = lax.axis_index("z"), lax.axis_index("x")
    side_index = lax.axis_index("y") * core_size + lax.axis_index("core")
    tok_rows, _ = attn_inputs.shape
    half = tok_rows // ROLLS
    full_len = half * z_size * PAIR
    shard_rows = first_moment.shape[0]
    y_index, core_index = lax.axis_index("y"), lax.axis_index("core")
    place = jnp.stack([z_index, x_index, y_index, core_index]).astype(jnp.int32)

    key_room, key_out, q_out, g_out = packed(key_vectors, queries, logp_grad)
    key_far = shift(key_out, "x", 1)
    q_far = shift(q_out, "x", 1)
    g_far = shift(g_out, "x", 1)
    key_block = lax.dynamic_update_slice(key_room, key_far, (tok_rows, 0))
    key_blocks = [key_block] + [shift(key_block, "z", k, False) for k in range(1, z_size)]
    columns = attn_inputs.T.reshape(z_size, PAIR, y_size, core_size, shard_rows, tok_rows)
    found = []
    block = (z_size, core_size, shard_rows, tok_rows)
    cuts = sliced(plane_kernel, place, [columns], [block] * (PAIR * y_size))
    for x in range(PAIR):
        for k in range(y_size):
            piece = cuts[x * y_size + k]
            if x or k:
                pairs = [
                    (a * y_size + b, (a + x) % PAIR * y_size + (b + k) % y_size)
                    for a in range(PAIR)
                    for b in range(y_size)
                ]
                piece = lax.ppermute(piece, ("x", "y"), pairs)
            found.append(piece)
    every = (PAIR * y_size, z_size, shard_rows, tok_rows)
    near_cols, far_cols = sliced(core_kernel, place, found, [every] * 2)
    far_cols = shift(far_cols, "core", 1)

    coeff = coefficients(
        place, rewards, group_ids, lengths, new_logp, old_logp, full_len
    )
    coeff_far = shift(coeff, "x", 1)

    own_proj = lax.dynamic_slice_in_dim(value_proj, side_index * shard_rows, shard_rows, 0)
    own_proj = lax.optimization_barrier(own_proj)
    bits = z_bits(z_size)
    known = own_proj[None]
    for n, bit in enumerate(bits):
        pairs = [(i, i ^ bit) for i in range(z_size)]
        arrived = lax.ppermute(known, "z", pairs)
        if n < len(bits) - 1:
            known = jnp.concatenate([known, arrived], axis=0)
    proj = [known, arrived, shift(known, "core", 1), shift(arrived, "core", 1)]

    parts = attention_parts(place, queries, q_far, logp_grad, g_far, coeff, coeff_far, key_blocks)
    total = parts[0].astype(jnp.float32)
    for k in range(1, z_size):
        arrived = shift(parts[k], "z", -k, False)
        total = total + arrived.astype(jnp.float32)

    def over_sides(value):
        found = [value] + [shift(value, "y", k) for k in range(1, y_size)]
        return found + [shift(block, "core", 1) for block in found]

    first_cols = total.astype(jnp.bfloat16)
    second_cols = shift(first_cols, "x", 1)
    first_all = over_sides(first_cols)
    second_all = over_sides(second_cols)

    pieces = owner_products(place, near_cols, far_cols, first_all, second_all)
    arrived_sums = [shift(pieces[k], "z", k) for k in range(1, z_size)]
    products = row_products(place, pieces[z_size], PAIR * y_size, proj)
    back = list(products)
    for k in range(1, y_size):
        back[k] = shift(products[k], "y", -k)
    back[y_size] = shift(products[y_size], "x", 1)
    for k in range(1, y_size):
        pairs = [
            (x * y_size + y, (1 - x) * y_size + (y - k) % y_size)
            for x in range(PAIR)
            for y in range(y_size)
        ]
        back[y_size + k] = lax.ppermute(products[y_size + k], ("x", "y"), pairs)
    input_grad = assembled(place, back, z_size)

    new_rows, new_first, new_second = adam_step(
        place, [pieces[0], *arrived_sums], own_proj, first_moment, second_moment
    )
    sides = [new_rows] + [shift(new_rows, "y", k) for k in range(1, y_size)]
    others = [shift(block, "core", 1) for block in sides]
    if y_size == 2:
        columns = [
            [jnp.where(y_index == 0, blocks[y], blocks[1 - y]) for y in range(2)]
            for blocks in (sides, others)
        ]
    else:
        columns = [list(by_place(blocks, y_index)) for blocks in (sides, others)]
    new_proj = jnp.concatenate(
        [
            jnp.where(core_index == c, columns[0][y], columns[1][y])
            for y in range(y_size)
            for c in range(core_size)
        ],
        axis=0,
    )
    return (input_grad, new_proj, new_first, new_second)


def solution(mesh):
    fsdp_size, side_size = mesh.shape["fsdp"], mesh.shape["side"]
    fine = Mesh(
        mesh.devices.reshape(fsdp_size // PAIR, PAIR, side_size // 2, 2),
        ("z", "x", "y", "core"),
    )
    tokens = ("y", "core", "z", "x")
    placed = (
        P(tokens, None),
        P(tokens, None),
        P(tokens, None),
        P(tokens, None),
        P(tokens),
        P(tokens),
        P(),
        P(),
        P(),
        P(("z", "x"), None),
        P(("z", "x", "y", "core"), None),
        P(("z", "x", "y", "core"), None),
    )
    return jax.shard_map(
        step,
        mesh=fine,
        in_specs=placed,
        out_specs=(
            P(tokens, None),
            P(("z", "x"), None),
            P(("z", "x", "y", "core"), None),
            P(("z", "x", "y", "core"), None),
        ),
        check_vma=False,
    )
```

profile of v0, /device:TPU:0, one launch (start us, length us, event | category | flops | bytes accessed | tf_op | source)
XLA Modules:
  0.0 100.4 jit_solution(8306635995303860889)
XLA Ops:
  0.7 2.2 %shard_map.149 = (bf16[256,256]{1,0:T(8,128)(2,1)}, bf16[128,256]{1,0:T(8,128)(2,1)}, bf16[128,1280]{1,0:T(8,128)(2,1)}, bf16[128,1280]{1,0:T(8,128)(2,1)}) custom-call(bf16[128,512]{1,0:T(8,128)(2,1)} %keys.1, bf16[128,2560]{1,0:T(8,128)(2,1)} %q_own.1, bf16[128,2560]{1,0:T(8,128)(2,1)} %g_own.1), custom_call_target="tpu_custom_call" | custom-call | bytes 1310720 | tf_op jit(solution)/shard_map/pallas_call | solution.py:194
  2.9 3.0 %collective-permute-start.7 = (bf16[128,256]{1,0:T(8,128)(2,1)}, bf16[128,256]{1,0:T(8,128)(2,1)S(1)}, u32[]{:S(2)}, u32[]{:S(2)}) collective-permute-start(bf16[128,256]{1,0:T(8,128)(2,1)} %get-tuple-element.39), channel_id=1, source_target_pairs={{0,4},{4,0},{1,5},{5,1},{2,6},{6,2},{3,7},{7,3},{8,12},{12,8},{9,1... | collective-permute-start | bytes 196616 | tf_op jit(solution)/shard_map/ppermute | solution.py:540
  6.1 2.7 %collective-permute-done.7 = bf16[128,256]{1,0:T(8,128)(2,1)S(1)} collective-permute-done((bf16[128,256]{1,0:T(8,128)(2,1)}, bf16[128,256]{1,0:T(8,128)(2,1)S(1)}, u32[]{:S(2)}, u32[]{:S(2)}) %collective-permute-start.7) | collective-permute-done | bytes 65568 | tf_op jit(solution)/shard_map/ppermute | solution.py:540
  8.8 0.6 constant_dynamic-update-slice_fusion.refs_0_
  9.4 4.3 %collective-permute-start.8 = (bf16[256,256]{1,0:T(8,128)(2,1)}, bf16[256,256]{1,0:T(8,128)(2,1)S(1)}, u32[]{:S(2)}, u32[]{:S(2)}) collective-permute-start(bf16[256,256]{1,0:T(8,128)(2,1)} %constant_dynamic-update-slice_fusion.refs_0_), channel_id=1, source_target_pairs={{0,8},{8,16},{16,24},{1,9},{9,17},{17,25},{2,10},{10,18},{18,26},{... | collective-permute-start | bytes 393224 | tf_op jit(solution)/shard_map/ppermute | solution.py:540
  13.7 4.5 %collective-permute-start.9 = (bf16[256,256]{1,0:T(8,128)(2,1)}, bf16[256,256]{1,0:T(8,128)(2,1)S(1)}, u32[]{:S(2)}, u32[]{:S(2)}) collective-permute-start(bf16[256,256]{1,0:T(8,128)(2,1)} %constant_dynamic-update-slice_fusion.refs_0_), channel_id=1, source_target_pairs={{0,16},{8,24},{1,17},{9,25},{2,18},{10,26},{3,19},{11,27},{4,20},{... | collective-permute-start | bytes 393224 | tf_op jit(solution)/shard_map/ppermute | solution.py:540
  18.2 1.9 %collective-permute-start.10 = (bf16[256,256]{1,0:T(8,128)(2,1)}, bf16[256,256]{1,0:T(8,128)(2,1)}, u32[]{:S(2)}, u32[]{:S(2)}) collective-permute-start(bf16[256,256]{1,0:T(8,128)(2,1)} %constant_dynamic-update-slice_fusion.refs_0_), channel_id=1, source_target_pairs={{0,24},{1,25},{2,26},{3,27},{4,28},{5,29},{6,30},{7,31}} | collective-permute-start | bytes 393224 | tf_op jit(solution)/shard_map/ppermute | solution.py:540
  20.3 0.6 shard_map.150.c_own
  20.9 1.6 %collective-permute-start.6 = (f32[1,128]{1,0:T(1,128)S(1)}, f32[1,128]{1,0:T(1,128)S(1)}, u32[]{:S(2)}, u32[]{:S(2)}) collective-permute-start(f32[1,128]{1,0:T(1,128)S(1)} %shard_map.150.c_own), channel_id=1, source_target_pairs={{0,4},{4,0},{1,5},{5,1},{2,6},{6,2},{3,7},{7,3},{8,12},{12,8},{9,1... | collective-permute-start | bytes 1544 | tf_op jit(solution)/shard_map/ppermute | solution.py:540
  22.5 2.0 %collective-permute-done.6.c_far = f32[1,128]{1,0:T(1,128)S(1)} collective-permute-done((f32[1,128]{1,0:T(1,128)S(1)}, f32[1,128]{1,0:T(1,128)S(1)}, u32[]{:S(2)}, u32[]{:S(2)}) %collective-permute-start.6) | collective-permute-done | bytes 544 | tf_op jit(solution)/shard_map/ppermute | solution.py:540
  24.5 1.6 %collective-permute-start.5 = (bf16[128,1280]{1,0:T(8,128)(2,1)}, bf16[128,1280]{1,0:T(8,128)(2,1)}, u32[]{:S(2)}, u32[]{:S(2)}) collective-permute-start(bf16[128,1280]{1,0:T(8,128)(2,1)} %get-tuple-element.37), channel_id=1, source_target_pairs={{0,4},{4,0},{1,5},{5,1},{2,6},{6,2},{3,7},{7,3},{8,12},{12,8},{9,1... | collective-permute-start | bytes 983048 | tf_op jit(solution)/shard_map/ppermute | solution.py:540
  26.1 0.8 copy.16
  26.9 1.6 %shard_map.147 = (bf16[4,2,160,128]{3,2,1,0:T(8,128)(2,1)S(1)}, bf16[4,2,160,128]{3,2,1,0:T(8,128)(2,1)}, bf16[4,2,160,128]{3,2,1,0:T(8,128)(2,1)}, bf16[4,2,160,128]{3,2,1,0:T(8,128)(2,1)}) custom-call(s32[4]{0:T(128)S(1)} %pad_add_fusion.place, bf16[4,2,2,2,160,128]{5,4,3,2,1,0:T(8,128)(2,1)S(1)} %bitcast.9), custom_call_target="tpu_custom_call" | custom-call | bytes 2621440 | tf_op jit(solution)/shard_map/pallas_call | solution.py:371
  28.5 0.7 copy-done.3
  29.2 1.5 %collective-permute-start = (bf16[4,2,160,128]{3,2,1,0:T(8,128)(2,1)}, bf16[4,2,160,128]{3,2,1,0:T(8,128)(2,1)S(1)}, u32[]{:S(2)}, u32[]{:S(2)}) collective-permute-start(bf16[4,2,160,128]{3,2,1,0:T(8,128)(2,1)} %get-tuple-element.31), channel_id=1, source_target_pairs={{0,2},{2,0},{4,6},{6,4},{1,3},{3,1},{5,7},{7,5},{8,10},{10,8},{12,... | collective-permute-start | bytes 983048 | tf_op jit(solution)/shard_map/ppermute | solution.py:608
  30.7 0.5 collective-permute-start.1
  31.2 1.5 %collective-permute-start.2 = (bf16[4,2,160,128]{3,2,1,0:T(8,128)(2,1)}, bf16[4,2,160,128]{3,2,1,0:T(8,128)(2,1)S(1)}, u32[]{:S(2)}, u32[]{:S(2)}) collective-permute-start(bf16[4,2,160,128]{3,2,1,0:T(8,128)(2,1)} %get-tuple-element.33), channel_id=1, source_target_pairs={{0,6},{2,4},{4,2},{6,0},{1,7},{3,5},{5,3},{7,1},{8,14},{10,12},{12... | collective-permute-start | bytes 983048 | tf_op jit(solution)/shard_map/ppermute | solution.py:608
  32.8 1.7 %collective-permute-done.5.g_far = bf16[128,1280]{1,0:T(8,128)(2,1)} collective-permute-done((bf16[128,1280]{1,0:T(8,128)(2,1)}, bf16[128,1280]{1,0:T(8,128)(2,1)}, u32[]{:S(2)}, u32[]{:S(2)}) %collective-permute-start.5) | collective-permute-done | bytes 327712 | tf_op jit(solution)/shard_map/ppermute | solution.py:540
  34.5 0.9 copy-done.12
  35.4 5.1 %shard_map.151 = (bf16[256,256]{1,0:T(8,128)(2,1)S(1)}, bf16[256,256]{1,0:T(8,128)(2,1)S(1)}, bf16[256,256]{1,0:T(8,128)(2,1)S(1)}, bf16[256,256]{1,0:T(8,128)(2,1)S(1)}) custom-call(s32[4]{0:T(128)S(1)} %pad_add_fusion.place, bf16[128,2560]{1,0:T(8,128)(2,1)S(1)} %copy-done.1, bf16[128,1280]{1,0:T(8,128)(2,1)} %collective-permute-done.4.q_far, ...), custom_call_target="tpu_custom_call" | custom-call | flops 671088640 | bytes 1310720 | tf_op jit(solution)/shard_map/pallas_call | solution.py:143
  40.5 1.3 %collective-permute-start.13 = (bf16[256,256]{1,0:T(8,128)(2,1)S(1)}, bf16[256,256]{1,0:T(8,128)(2,1)S(1)}, u32[]{:S(2)}, u32[]{:S(2)}) collective-permute-start(bf16[256,256]{1,0:T(8,128)(2,1)S(1)} %get-tuple-element.43), channel_id=1, source_target_pairs={{24,0},{25,1},{26,2},{27,3},{28,4},{29,5},{30,6},{31,7}} | collective-permute-start | bytes 393224 | tf_op jit(solution)/shard_map/ppermute | solution.py:540
  41.8 1.3 %collective-permute-start.12 = (bf16[256,256]{1,0:T(8,128)(2,1)S(1)}, bf16[256,256]{1,0:T(8,128)(2,1)S(1)}, u32[]{:S(2)}, u32[]{:S(2)}) collective-permute-start(bf16[256,256]{1,0:T(8,128)(2,1)S(1)} %get-tuple-element.42), channel_id=1, source_target_pairs={{16,0},{24,8},{17,1},{25,9},{18,2},{26,10},{19,3},{27,11},{20,4},{... | collective-permute-start | bytes 393224 | tf_op jit(solution)/shard_map/ppermute | solution.py:540
  43.1 1.3 %collective-permute-start.11 = (bf16[256,256]{1,0:T(8,128)(2,1)S(1)}, bf16[256,256]{1,0:T(8,128)(2,1)S(1)}, u32[]{:S(2)}, u32[]{:S(2)}) collective-permute-start(bf16[256,256]{1,0:T(8,128)(2,1)S(1)} %get-tuple-element.41), channel_id=1, source_target_pairs={{8,0},{16,8},{24,16},{9,1},{17,9},{25,17},{10,2},{18,10},{26,18},{... | collective-permute-start | bytes 393224 | tf_op jit(solution)/shard_map/ppermute | solution.py:540
  44.4 2.3 %collective-permute-done.2.refs_3_ = bf16[4,2,160,128]{3,2,1,0:T(8,128)(2,1)S(1)} collective-permute-done((bf16[4,2,160,128]{3,2,1,0:T(8,128)(2,1)}, bf16[4,2,160,128]{3,2,1,0:T(8,128)(2,1)S(1)}, u32[]{:S(2)}, u32[]{:S(2)}) %collective-permute-start.2) | collective-permute-done | bytes 327712 | tf_op jit(solution)/shard_map/ppermute | solution.py:608
  46.7 0.6 shard_map.148
  47.5 0.4 collective-permute-start.22
  47.9 1.4 %collective-permute-done.13 = bf16[256,256]{1,0:T(8,128)(2,1)S(1)} collective-permute-done((bf16[256,256]{1,0:T(8,128)(2,1)S(1)}, bf16[256,256]{1,0:T(8,128)(2,1)S(1)}, u32[]{:S(2)}, u32[]{:S(2)}) %collective-permute-start.13) | collective-permute-done | bytes 131104 | tf_op jit(solution)/shard_map/ppermute | solution.py:540
  49.3 2.7 %collective-permute-done.12 = bf16[256,256]{1,0:T(8,128)(2,1)S(1)} collective-permute-done((bf16[256,256]{1,0:T(8,128)(2,1)S(1)}, bf16[256,256]{1,0:T(8,128)(2,1)S(1)}, u32[]{:S(2)}, u32[]{:S(2)}) %collective-permute-start.12) | collective-permute-done | bytes 131104 | tf_op jit(solution)/shard_map/ppermute | solution.py:540
  52.1 3.7 %collective-permute-start.14 = (bf16[256,256]{1,0:T(8,128)(2,1)S(1)}, bf16[256,256]{1,0:T(8,128)(2,1)S(1)}, u32[]{:S(2)}, u32[]{:S(2)}) collective-permute-start(bf16[256,256]{1,0:T(8,128)(2,1)S(1)} %add_convert_fusion.refs_0_), channel_id=1, source_target_pairs={{0,2},{2,0},{1,3},{3,1},{4,6},{6,4},{5,7},{7,5},{8,10},{10,8},{9,1... | collective-permute-start | bytes 393224 | tf_op jit(solution)/shard_map/ppermute | solution.py:540
  55.9 1.6 %collective-permute-start.17 = (bf16[256,256]{1,0:T(8,128)(2,1)S(1)}, bf16[256,256]{1,0:T(8,128)(2,1)S(1)}, u32[]{:S(2)}, u32[]{:S(2)}) collective-permute-start(bf16[256,256]{1,0:T(8,128)(2,1)S(1)} %add_convert_fusion.refs_0_), channel_id=1, source_target_pairs={{0,4},{4,0},{1,5},{5,1},{2,6},{6,2},{3,7},{7,3},{8,12},{12,8},{9,1... | collective-permute-start | bytes 393224 | tf_op jit(solution)/shard_map/ppermute | solution.py:540
  57.4 1.4 %collective-permute-done.14.refs_1_ = bf16[256,256]{1,0:T(8,128)(2,1)S(1)} collective-permute-done((bf16[256,256]{1,0:T(8,128)(2,1)S(1)}, bf16[256,256]{1,0:T(8,128)(2,1)S(1)}, u32[]{:S(2)}, u32[]{:S(2)}) %collective-permute-start.14) | collective-permute-done | bytes 131104 | tf_op jit(solution)/shard_map/ppermute | solution.py:540
  58.8 2.0 %collective-permute-done.17.refs_4_ = bf16[256,256]{1,0:T(8,128)(2,1)S(1)} collective-permute-done((bf16[256,256]{1,0:T(8,128)(2,1)S(1)}, bf16[256,256]{1,0:T(8,128)(2,1)S(1)}, u32[]{:S(2)}, u32[]{:S(2)}) %collective-permute-start.17) | collective-permute-done | bytes 131104 | tf_op jit(solution)/shard_map/ppermute | solution.py:540
  61.6 4.2 %collective-permute-done.18.refs_5_ = bf16[256,256]{1,0:T(8,128)(2,1)S(1)} collective-permute-done((bf16[256,256]{1,0:T(8,128)(2,1)S(1)}, bf16[256,256]{1,0:T(8,128)(2,1)S(1)}, u32[]{:S(2)}, u32[]{:S(2)}) %collective-permute-start.18) | collective-permute-done | bytes 131104 | tf_op jit(solution)/shard_map/ppermute | solution.py:540
  65.8 1.3 %collective-permute-done.20.refs_7_ = bf16[256,256]{1,0:T(8,128)(2,1)S(1)} collective-permute-done((bf16[256,256]{1,0:T(8,128)(2,1)S(1)}, bf16[256,256]{1,0:T(8,128)(2,1)S(1)}, u32[]{:S(2)}, u32[]{:S(2)}) %collective-permute-start.20) | collective-permute-done | bytes 131104 | tf_op jit(solution)/shard_map/ppermute | solution.py:540
  67.2 2.0 %shard_map.152 = (bf16[160,512]{1,0:T(8,128)(2,1)S(1)}, bf16[160,512]{1,0:T(8,128)(2,1)S(1)}, bf16[160,512]{1,0:T(8,128)(2,1)S(1)}, bf16[160,512]{1,0:T(8,128)(2,1)S(1)}, bf16[512,512]{1,0:T(8,128)(2,1)S(1)}) custom-call(s32[4]{0:T(128)S(1)} %pad_add_fusion.place, bf16[4,4,160,128]{3,2,1,0:T(8,128)(2,1)S(1)} %get-tuple-element.34.near, ...), custom_call_target="tpu_custom_call" | custom-call | flops 671088640 | bytes 2621440 | tf_op jit(solution)/shard_map/pallas_call | solution.py:298
  69.2 0.7 collective-permute-start.28
  70.2 2.8 %collective-permute-start.30 = (bf16[160,512]{1,0:T(8,128)(2,1)S(1)}, bf16[160,512]{1,0:T(8,128)(2,1)S(1)}, u32[]{:S(2)}, u32[]{:S(2)}) collective-permute-start(bf16[160,512]{1,0:T(8,128)(2,1)S(1)} %get-tuple-element.52), channel_id=1, source_target_pairs={{0,24},{8,0},{16,8},{24,16},{1,25},{9,1},{17,9},{25,17},{2,26},{10... | collective-permute-start | bytes 491528 | tf_op jit(solution)/shard_map/ppermute | solution.py:540
  73.1 3.2 %shard_map.153 = (bf16[128,1280]{1,0:T(8,128)(2,1)S(1)}, bf16[128,1280]{1,0:T(8,128)(2,1)S(1)}, bf16[128,1280]{1,0:T(8,128)(2,1)S(1)}, bf16[128,1280]{1,0:T(8,128)(2,1)S(1)}) custom-call(s32[4]{0:T(128)S(1)} %pad_add_fusion.place, bf16[512,512]{1,0:T(8,128)(2,1)S(1)} %get-tuple-element.44.token_rows, bf16[2,160,512]{2,1,0:T(8,128)(2,1)S(1)} %pad_maximum_fusion.1.refs_0_, ...), custom_call_target="tpu_custom_call" | custom-call | flops 671088640 | bytes 2621440 | tf_op jit(solution)/shard_map/pallas_call | solution.py:415
  76.3 1.0 %collective-permute-start.25 = (bf16[128,1280]{1,0:T(8,128)(2,1)S(1)}, bf16[128,1280]{1,0:T(8,128)(2,1)S(1)}, u32[]{:S(2)}, u32[]{:S(2)}) collective-permute-start(bf16[128,1280]{1,0:T(8,128)(2,1)S(1)} %get-tuple-element.46), channel_id=1, source_target_pairs={{0,2},{2,0},{1,3},{3,1},{4,6},{6,4},{5,7},{7,5},{8,10},{10,8},{9,1... | collective-permute-start | bytes 983048 | tf_op jit(solution)/shard_map/ppermute | solution.py:540
  77.3 1.6 %collective-permute-start.26 = (bf16[128,1280]{1,0:T(8,128)(2,1)S(1)}, bf16[128,1280]{1,0:T(8,128)(2,1)S(1)}, u32[]{:S(2)}, u32[]{:S(2)}) collective-permute-start(bf16[128,1280]{1,0:T(8,128)(2,1)S(1)} %get-tuple-element.47), channel_id=1, source_target_pairs={{0,4},{4,0},{1,5},{5,1},{2,6},{6,2},{3,7},{7,3},{8,12},{12,8},{9,1... | collective-permute-start | bytes 983048 | tf_op jit(solution)/shard_map/ppermute | solution.py:540
  78.9 1.3 %collective-permute-start.27 = (bf16[128,1280]{1,0:T(8,128)(2,1)S(1)}, bf16[128,1280]{1,0:T(8,128)(2,1)S(1)}, u32[]{:S(2)}, u32[]{:S(2)}) collective-permute-start(bf16[128,1280]{1,0:T(8,128)(2,1)S(1)} %get-tuple-element.48), channel_id=1, source_target_pairs={{0,6},{2,4},{4,2},{6,0},{1,7},{3,5},{5,3},{7,1},{8,14},{10,12},{12... | collective-permute-start | bytes 983048 | tf_op jit(solution)/shard_map/ppermute | solution.py:658
  80.2 4.2 %collective-permute-done.29.refs_2_ = bf16[160,512]{1,0:T(8,128)(2,1)S(1)} collective-permute-done((bf16[160,512]{1,0:T(8,128)(2,1)S(1)}, bf16[160,512]{1,0:T(8,128)(2,1)S(1)}, u32[]{:S(2)}, u32[]{:S(2)}) %collective-permute-start.29) | collective-permute-done | bytes 163872 | tf_op jit(solution)/shard_map/ppermute | solution.py:540
  84.4 1.5 %shard_map.155 = (bf16[160,512]{1,0:T(8,128)(2,1)S(1)}, bf16[160,512]{1,0:T(8,128)(2,1)}, bf16[160,512]{1,0:T(8,128)(2,1)}) custom-call(s32[4]{0:T(128)S(1)} %pad_add_fusion.place, bf16[160,512]{1,0:T(8,128)(2,1)S(1)} %get-tuple-element.49.refs_0_, bf16[160,512]{1,0:T(8,128)(2,1)S(1)} %collective-permute-done.28.refs_1_, ...), custom_call_target="tpu_custom_call" | custom-call | flops 3276800 | bytes 1638400 | tf_op jit(solution)/shard_map/pallas_call | solution.py:523
  85.9 0.9 collective-permute-start.31
  86.9 9.9 %collective-permute-done.31 = bf16[160,512]{1,0:T(8,128)(2,1)S(1)} collective-permute-done((bf16[160,512]{1,0:T(8,128)(2,1)S(1)}, bf16[160,512]{1,0:T(8,128)(2,1)S(1)}, u32[]{:S(2)}, u32[]{:S(2)}) %collective-permute-start.31) | collective-permute-done | bytes 163872 | tf_op jit(solution)/shard_map/ppermute | solution.py:540
  96.8 1.8 %shard_map.154 = bf16[128,5120]{1,0:T(8,128)(2,1)} custom-call(s32[4]{0:T(128)S(1)} %pad_add_fusion.place, bf16[128,1280]{1,0:T(8,128)(2,1)S(1)} %get-tuple-element.45.refs_0_, bf16[128,1280]{1,0:T(8,128)(2,1)S(1)} %collective-permute-done.25.refs_1_, bf16[128,1280]{1,0:T(8,128)(2,1)S(1)} %collective-permute-done.26.refs_2_, ...), custom_call_target="tpu_custom_call" | custom-call | bytes 2621440 | tf_op jit(solution)/shard_map/pallas_call | solution.py:473
  98.6 1.0 broadcast_select_fusion.7
  99.6 0.9 pad_maximum_fusion
  (65 shorter events, 1.7 us)
Async XLA Ops:
  0.6 32.0 %copy-start = (bf16[640,512]{1,0:T(8,128)(2,1)S(1)}, bf16[640,512]{1,0:T(8,128)(2,1)}, u32[]{:S(2)}) copy-start(bf16[640,512]{1,0:T(8,128)(2,1)} %param.21) | copy-start | bytes 1966084
  0.6 19.6 %copy-start.7 = (f32[8]{0:T(128)S(1)}, f32[8]{0:T(128)}, u32[]{:S(2)}) copy-start(f32[8]{0:T(128)} %rewards.1) | copy-start | bytes 100
  0.7 19.6 %copy-start.8 = (s32[8]{0:T(128)S(1)}, s32[8]{0:T(128)}, u32[]{:S(2)}) copy-start(s32[8]{0:T(128)} %group_ids.1) | copy-start | bytes 100
  0.7 19.6 %copy-start.9 = (s32[8]{0:T(128)S(1)}, s32[8]{0:T(128)}, u32[]{:S(2)}) copy-start(s32[8]{0:T(128)} %lengths.1) | copy-start | bytes 100
  0.7 19.6 %copy-start.10 = (f32[128]{0:T(128)S(1)}, f32[128]{0:T(128)}, u32[]{:S(2)}) copy-start(f32[128]{0:T(128)} %param.16) | copy-start | bytes 1540
  0.7 19.6 %copy-start.11 = (f32[128]{0:T(128)S(1)}, f32[128]{0:T(128)}, u32[]{:S(2)}) copy-start(f32[128]{0:T(128)} %param.17) | copy-start | bytes 1540
  0.7 25.4 %copy-start.13 = (bf16[128,5120]{1,0:T(8,128)(2,1)S(1)}, bf16[128,5120]{1,0:T(8,128)(2,1)}, u32[]{:S(2)}) copy-start(bf16[128,5120]{1,0:T(8,128)(2,1)} %param.12) | copy-start | bytes 3932164
  2.9 5.8 %collective-permute-start.7 = (bf16[128,256]{1,0:T(8,128)(2,1)}, bf16[128,256]{1,0:T(8,128)(2,1)S(1)}, u32[]{:S(2)}, u32[]{:S(2)}) collective-permute-start(bf16[128,256]{1,0:T(8,128)(2,1)} %get-tuple-element.39), channel_id=1, source_target_pairs={{0,4},{4,0},{1,5},{5,1},{2,6},{6,2},{3,7},{7,3},{8,12},{12,8},{9,1... | collective-permute-start | bytes 196616 | tf_op jit(solution)/shard_map/ppermute | solution.py:540
  6.0 26.7 %collective-permute-start.4 = (bf16[128,1280]{1,0:T(8,128)(2,1)}, bf16[128,1280]{1,0:T(8,128)(2,1)}, u32[]{:S(2)}, u32[]{:S(2)}) collective-permute-start(bf16[128,1280]{1,0:T(8,128)(2,1)} %get-tuple-element.36), channel_id=1, source_target_pairs={{0,4},{4,0},{1,5},{5,1},{2,6},{6,2},{3,7},{7,3},{8,12},{12,8},{9,1... | collective-permute-start | bytes 983048 | tf_op jit(solution)/shard_map/ppermute | solution.py:540
  9.4 19.8 %collective-permute-start.8 = (bf16[256,256]{1,0:T(8,128)(2,1)}, bf16[256,256]{1,0:T(8,128)(2,1)S(1)}, u32[]{:S(2)}, u32[]{:S(2)}) collective-permute-start(bf16[256,256]{1,0:T(8,128)(2,1)} %constant_dynamic-update-slice_fusion.refs_0_), channel_id=1, source_target_pairs={{0,8},{8,16},{16,24},{1,9},{9,17},{17,25},{2,10},{10,18},{18,26},{... | collective-permute-start | bytes 393224 | tf_op jit(solution)/shard_map/ppermute | solution.py:540
  13.7 17.0 %collective-permute-start.9 = (bf16[256,256]{1,0:T(8,128)(2,1)}, bf16[256,256]{1,0:T(8,128)(2,1)S(1)}, u32[]{:S(2)}, u32[]{:S(2)}) collective-permute-start(bf16[256,256]{1,0:T(8,128)(2,1)} %constant_dynamic-update-slice_fusion.refs_0_), channel_id=1, source_target_pairs={{0,16},{8,24},{1,17},{9,25},{2,18},{10,26},{3,19},{11,27},{4,20},{... | collective-permute-start | bytes 393224 | tf_op jit(solution)/shard_map/ppermute | solution.py:540
  18.2 13.0 %collective-permute-start.10 = (bf16[256,256]{1,0:T(8,128)(2,1)}, bf16[256,256]{1,0:T(8,128)(2,1)}, u32[]{:S(2)}, u32[]{:S(2)}) collective-permute-start(bf16[256,256]{1,0:T(8,128)(2,1)} %constant_dynamic-update-slice_fusion.refs_0_), channel_id=1, source_target_pairs={{0,24},{1,25},{2,26},{3,27},{4,28},{5,29},{6,30},{7,31}} | collective-permute-start | bytes 393224 | tf_op jit(solution)/shard_map/ppermute | solution.py:540
  20.9 3.6 %collective-permute-start.6 = (f32[1,128]{1,0:T(1,128)S(1)}, f32[1,128]{1,0:T(1,128)S(1)}, u32[]{:S(2)}, u32[]{:S(2)}) collective-permute-start(f32[1,128]{1,0:T(1,128)S(1)} %shard_map.150.c_own), channel_id=1, source_target_pairs={{0,4},{4,0},{1,5},{5,1},{2,6},{6,2},{3,7},{7,3},{8,12},{12,8},{9,1... | collective-permute-start | bytes 1544 | tf_op jit(solution)/shard_map/ppermute | solution.py:540
  24.5 10.0 %collective-permute-start.5 = (bf16[128,1280]{1,0:T(8,128)(2,1)}, bf16[128,1280]{1,0:T(8,128)(2,1)}, u32[]{:S(2)}, u32[]{:S(2)}) collective-permute-start(bf16[128,1280]{1,0:T(8,128)(2,1)} %get-tuple-element.37), channel_id=1, source_target_pairs={{0,4},{4,0},{1,5},{5,1},{2,6},{6,2},{3,7},{7,3},{8,12},{12,8},{9,1... | collective-permute-start | bytes 983048 | tf_op jit(solution)/shard_map/ppermute | solution.py:540
  26.9 7.6 %copy-start.1 = (bf16[128,2560]{1,0:T(8,128)(2,1)S(1)}, bf16[128,2560]{1,0:T(8,128)(2,1)}, u32[]{:S(2)}) copy-start(bf16[128,2560]{1,0:T(8,128)(2,1)} %q_own.1) | copy-start | bytes 1966084
  26.9 7.6 %copy-start.2 = (bf16[128,2560]{1,0:T(8,128)(2,1)S(1)}, bf16[128,2560]{1,0:T(8,128)(2,1)}, u32[]{:S(2)}) copy-start(bf16[128,2560]{1,0:T(8,128)(2,1)} %g_own.1) | copy-start | bytes 1966084
  28.5 0.7 copy-start.3
  29.2 12.6 %collective-permute-start = (bf16[4,2,160,128]{3,2,1,0:T(8,128)(2,1)}, bf16[4,2,160,128]{3,2,1,0:T(8,128)(2,1)S(1)}, u32[]{:S(2)}, u32[]{:S(2)}) collective-permute-start(bf16[4,2,160,128]{3,2,1,0:T(8,128)(2,1)} %get-tuple-element.31), channel_id=1, source_target_pairs={{0,2},{2,0},{4,6},{6,4},{1,3},{3,1},{5,7},{7,5},{8,10},{10,8},{12,... | collective-permute-start | bytes 983048 | tf_op jit(solution)/shard_map/ppermute | solution.py:608
  30.7 12.4 %collective-permute-start.1 = (bf16[4,2,160,128]{3,2,1,0:T(8,128)(2,1)}, bf16[4,2,160,128]{3,2,1,0:T(8,128)(2,1)S(1)}, u32[]{:S(2)}, u32[]{:S(2)}) collective-permute-start(bf16[4,2,160,128]{3,2,1,0:T(8,128)(2,1)} %get-tuple-element.32), channel_id=1, source_target_pairs={{0,4},{2,6},{4,0},{6,2},{1,5},{3,7},{5,1},{7,3},{8,12},{10,14},{12... | collective-permute-start | bytes 983048 | tf_op jit(solution)/shard_map/ppermute | solution.py:608
  31.2 15.5 %collective-permute-start.2 = (bf16[4,2,160,128]{3,2,1,0:T(8,128)(2,1)}, bf16[4,2,160,128]{3,2,1,0:T(8,128)(2,1)S(1)}, u32[]{:S(2)}, u32[]{:S(2)}) collective-permute-start(bf16[4,2,160,128]{3,2,1,0:T(8,128)(2,1)} %get-tuple-element.33), channel_id=1, source_target_pairs={{0,6},{2,4},{4,2},{6,0},{1,7},{3,5},{5,3},{7,1},{8,14},{10,12},{12... | collective-permute-start | bytes 983048 | tf_op jit(solution)/shard_map/ppermute | solution.py:608
  32.7 14.0 %copy-start.4 = (bf16[4,2,160,128]{3,2,1,0:T(8,128)(2,1)S(1)}, bf16[4,2,160,128]{3,2,1,0:T(8,128)(2,1)}, u32[]{:S(2)}) copy-start(bf16[4,2,160,128]{3,2,1,0:T(8,128)(2,1)} %copy-done.3) | copy-start | bytes 983044
  32.7 14.7 %collective-permute-start.21 = (bf16[1,160,512]{2,1,0:T(8,128)(2,1)S(1)}, bf16[1,160,512]{2,1,0:T(8,128)(2,1)S(1)}, u32[]{:S(2)}, u32[]{:S(2)}) collective-permute-start(bf16[1,160,512]{2,1,0:T(8,128)(2,1)S(1)} %bitcast.10), channel_id=1, source_target_pairs={{0,16},{8,24},{16,0},{24,8},{1,17},{9,25},{17,1},{25,9},{2,18},{10... | collective-permute-start | bytes 491528 | tf_op jit(solution)/shard_map/ppermute | solution.py:625
  34.5 0.9 copy-start.12
  40.5 8.8 %collective-permute-start.13 = (bf16[256,256]{1,0:T(8,128)(2,1)S(1)}, bf16[256,256]{1,0:T(8,128)(2,1)S(1)}, u32[]{:S(2)}, u32[]{:S(2)}) collective-permute-start(bf16[256,256]{1,0:T(8,128)(2,1)S(1)} %get-tuple-element.43), channel_id=1, source_target_pairs={{24,0},{25,1},{26,2},{27,3},{28,4},{29,5},{30,6},{31,7}} | collective-permute-start | bytes 393224 | tf_op jit(solution)/shard_map/ppermute | solution.py:540
  41.8 10.3 %collective-permute-start.12 = (bf16[256,256]{1,0:T(8,128)(2,1)S(1)}, bf16[256,256]{1,0:T(8,128)(2,1)S(1)}, u32[]{:S(2)}, u32[]{:S(2)}) collective-permute-start(bf16[256,256]{1,0:T(8,128)(2,1)S(1)} %get-tuple-element.42), channel_id=1, source_target_pairs={{16,0},{24,8},{17,1},{25,9},{18,2},{26,10},{19,3},{27,11},{20,4},{... | collective-permute-start | bytes 393224 | tf_op jit(solution)/shard_map/ppermute | solution.py:540
  43.1 8.9 %collective-permute-start.11 = (bf16[256,256]{1,0:T(8,128)(2,1)S(1)}, bf16[256,256]{1,0:T(8,128)(2,1)S(1)}, u32[]{:S(2)}, u32[]{:S(2)}) collective-permute-start(bf16[256,256]{1,0:T(8,128)(2,1)S(1)} %get-tuple-element.41), channel_id=1, source_target_pairs={{8,0},{16,8},{24,16},{9,1},{17,9},{25,17},{10,2},{18,10},{26,18},{... | collective-permute-start | bytes 393224 | tf_op jit(solution)/shard_map/ppermute | solution.py:540
  47.4 19.8 %collective-permute-start.3 = (bf16[4,4,160,128]{3,2,1,0:T(8,128)(2,1)S(1)}, bf16[4,4,160,128]{3,2,1,0:T(8,128)(2,1)S(1)}, u32[]{:S(2)}, u32[]{:S(2)}) collective-permute-start(bf16[4,4,160,128]{3,2,1,0:T(8,128)(2,1)S(1)} %get-tuple-element.35), channel_id=1, source_target_pairs={{0,1},{1,0},{2,3},{3,2},{4,5},{5,4},{6,7},{7,6},{8,9},{9,8},{10,11... | collective-permute-start | bytes 1966088 | tf_op jit(solution)/shard_map/ppermute | solution.py:540
  47.5 13.4 %collective-permute-start.22 = (bf16[2,160,512]{2,1,0:T(8,128)(2,1)S(1)}, bf16[2,160,512]{2,1,0:T(8,128)(2,1)S(1)}, u32[]{:S(2)}, u32[]{:S(2)}) collective-permute-start(bf16[2,160,512]{2,1,0:T(8,128)(2,1)S(1)} %pad_maximum_fusion.1.refs_0_), channel_id=1, source_target_pairs={{0,8},{8,0},{16,24},{24,16},{1,9},{9,1},{17,25},{25,17},{2,10},{10... | collective-permute-start | bytes 983048 | tf_op jit(solution)/shard_map/ppermute | solution.py:625
  52.1 6.7 %collective-permute-start.14 = (bf16[256,256]{1,0:T(8,128)(2,1)S(1)}, bf16[256,256]{1,0:T(8,128)(2,1)S(1)}, u32[]{:S(2)}, u32[]{:S(2)}) collective-permute-start(bf16[256,256]{1,0:T(8,128)(2,1)S(1)} %add_convert_fusion.refs_0_), channel_id=1, source_target_pairs={{0,2},{2,0},{1,3},{3,1},{4,6},{6,4},{5,7},{7,5},{8,10},{10,8},{9,1... | collective-permute-start | bytes 393224 | tf_op jit(solution)/shard_map/ppermute | solution.py:540
  55.9 5.0 %collective-permute-start.17 = (bf16[256,256]{1,0:T(8,128)(2,1)S(1)}, bf16[256,256]{1,0:T(8,128)(2,1)S(1)}, u32[]{:S(2)}, u32[]{:S(2)}) collective-permute-start(bf16[256,256]{1,0:T(8,128)(2,1)S(1)} %add_convert_fusion.refs_0_), channel_id=1, source_target_pairs={{0,4},{4,0},{1,5},{5,1},{2,6},{6,2},{3,7},{7,3},{8,12},{12,8},{9,1... | collective-permute-start | bytes 393224 | tf_op jit(solution)/shard_map/ppermute | solution.py:540
  57.4 3.6 %collective-permute-start.15 = (bf16[256,256]{1,0:T(8,128)(2,1)S(1)}, bf16[256,256]{1,0:T(8,128)(2,1)S(1)}, u32[]{:S(2)}, u32[]{:S(2)}) collective-permute-start(bf16[256,256]{1,0:T(8,128)(2,1)S(1)} %add_convert_fusion.refs_0_), channel_id=1, source_target_pairs={{0,1},{1,0},{2,3},{3,2},{4,5},{5,4},{6,7},{7,6},{8,9},{9,8},{10,11... | collective-permute-start | bytes 393224 | tf_op jit(solution)/shard_map/ppermute | solution.py:540
  58.8 2.6 %collective-permute-start.16 = (bf16[256,256]{1,0:T(8,128)(2,1)S(1)}, bf16[256,256]{1,0:T(8,128)(2,1)S(1)}, u32[]{:S(2)}, u32[]{:S(2)}) collective-permute-start(bf16[256,256]{1,0:T(8,128)(2,1)S(1)} %collective-permute-done.14.refs_1_), channel_id=1, source_target_pairs={{0,1},{1,0},{2,3},{3,2},{4,5},{5,4},{6,7},{7,6},{8,9},{9,8},{10,11... | collective-permute-start | bytes 393224 | tf_op jit(solution)/shard_map/ppermute | solution.py:540
  60.8 5.0 %collective-permute-start.18 = (bf16[256,256]{1,0:T(8,128)(2,1)S(1)}, bf16[256,256]{1,0:T(8,128)(2,1)S(1)}, u32[]{:S(2)}, u32[]{:S(2)}) collective-permute-start(bf16[256,256]{1,0:T(8,128)(2,1)S(1)} %collective-permute-done.17.refs_4_), channel_id=1, source_target_pairs={{0,2},{2,0},{1,3},{3,1},{4,6},{6,4},{5,7},{7,5},{8,10},{10,8},{9,1... | collective-permute-start | bytes 393224 | tf_op jit(solution)/shard_map/ppermute | solution.py:540
  60.9 12.2 %collective-permute-start.23 = (bf16[2,160,512]{2,1,0:T(8,128)(2,1)S(1)}, bf16[2,160,512]{2,1,0:T(8,128)(2,1)S(1)}, u32[]{:S(2)}, u32[]{:S(2)}) collective-permute-start(bf16[2,160,512]{2,1,0:T(8,128)(2,1)S(1)} %pad_maximum_fusion.1.refs_0_), channel_id=1, source_target_pairs={{0,1},{1,0},{2,3},{3,2},{4,5},{5,4},{6,7},{7,6},{8,9},{9,8},{10,11... | collective-permute-start | bytes 983048 | tf_op jit(solution)/shard_map/ppermute | solution.py:540
  61.1 12.0 %collective-permute-start.24 = (bf16[2,160,512]{2,1,0:T(8,128)(2,1)S(1)}, bf16[2,160,512]{2,1,0:T(8,128)(2,1)S(1)}, u32[]{:S(2)}, u32[]{:S(2)}) collective-permute-start(bf16[2,160,512]{2,1,0:T(8,128)(2,1)S(1)} %collective-permute-done.22.refs_1_), channel_id=1, source_target_pairs={{0,1},{1,0},{2,3},{3,2},{4,5},{5,4},{6,7},{7,6},{8,9},{9,8},{10,11... | collective-permute-start | bytes 983048 | tf_op jit(solution)/shard_map/ppermute | solution.py:540
  61.4 4.4 %collective-permute-start.19 = (bf16[256,256]{1,0:T(8,128)(2,1)S(1)}, bf16[256,256]{1,0:T(8,128)(2,1)S(1)}, u32[]{:S(2)}, u32[]{:S(2)}) collective-permute-start(bf16[256,256]{1,0:T(8,128)(2,1)S(1)} %collective-permute-done.17.refs_4_), channel_id=1, source_target_pairs={{0,1},{1,0},{2,3},{3,2},{4,5},{5,4},{6,7},{7,6},{8,9},{9,8},{10,11... | collective-permute-start | bytes 393224 | tf_op jit(solution)/shard_map/ppermute | solution.py:540
  65.8 1.3 %collective-permute-start.20 = (bf16[256,256]{1,0:T(8,128)(2,1)S(1)}, bf16[256,256]{1,0:T(8,128)(2,1)S(1)}, u32[]{:S(2)}, u32[]{:S(2)}) collective-permute-start(bf16[256,256]{1,0:T(8,128)(2,1)S(1)} %collective-permute-done.18.refs_5_), channel_id=1, source_target_pairs={{0,1},{1,0},{2,3},{3,2},{4,5},{5,4},{6,7},{7,6},{8,9},{9,8},{10,11... | collective-permute-start | bytes 393224 | tf_op jit(solution)/shard_map/ppermute | solution.py:540
  69.1 15.3 %copy-start.5 = (bf16[160,512]{1,0:T(8,128)(2,1)S(1)}, bf16[160,512]{1,0:T(8,128)(2,1)}, u32[]{:S(2)}) copy-start(bf16[160,512]{1,0:T(8,128)(2,1)} %refs_5_.1) | copy-start | bytes 491524
  69.1 15.3 %copy-start.6 = (bf16[160,512]{1,0:T(8,128)(2,1)S(1)}, bf16[160,512]{1,0:T(8,128)(2,1)}, u32[]{:S(2)}) copy-start(bf16[160,512]{1,0:T(8,128)(2,1)} %refs_6_.1) | copy-start | bytes 491524
  69.2 9.7 %collective-permute-start.28 = (bf16[160,512]{1,0:T(8,128)(2,1)S(1)}, bf16[160,512]{1,0:T(8,128)(2,1)S(1)}, u32[]{:S(2)}, u32[]{:S(2)}) collective-permute-start(bf16[160,512]{1,0:T(8,128)(2,1)S(1)} %get-tuple-element.50), channel_id=1, source_target_pairs={{0,8},{8,16},{16,24},{24,0},{1,9},{9,17},{17,25},{25,1},{2,10},{10... | collective-permute-start | bytes 491528 | tf_op jit(solution)/shard_map/ppermute | solution.py:540
  69.9 14.5 %collective-permute-start.29 = (bf16[160,512]{1,0:T(8,128)(2,1)S(1)}, bf16[160,512]{1,0:T(8,128)(2,1)S(1)}, u32[]{:S(2)}, u32[]{:S(2)}) collective-permute-start(bf16[160,512]{1,0:T(8,128)(2,1)S(1)} %get-tuple-element.51), channel_id=1, source_target_pairs={{0,16},{8,24},{16,0},{24,8},{1,17},{9,25},{17,1},{25,9},{2,18},{10... | collective-permute-start | bytes 491528 | tf_op jit(solution)/shard_map/ppermute | solution.py:540
  70.2 14.2 %collective-permute-start.30 = (bf16[160,512]{1,0:T(8,128)(2,1)S(1)}, bf16[160,512]{1,0:T(8,128)(2,1)S(1)}, u32[]{:S(2)}, u32[]{:S(2)}) collective-permute-start(bf16[160,512]{1,0:T(8,128)(2,1)S(1)} %get-tuple-element.52), channel_id=1, source_target_pairs={{0,24},{8,0},{16,8},{24,16},{1,25},{9,1},{17,9},{25,17},{2,26},{10... | collective-permute-start | bytes 491528 | tf_op jit(solution)/shard_map/ppermute | solution.py:540
  76.3 20.4 %collective-permute-start.25 = (bf16[128,1280]{1,0:T(8,128)(2,1)S(1)}, bf16[128,1280]{1,0:T(8,128)(2,1)S(1)}, u32[]{:S(2)}, u32[]{:S(2)}) collective-permute-start(bf16[128,1280]{1,0:T(8,128)(2,1)S(1)} %get-tuple-element.46), channel_id=1, source_target_pairs={{0,2},{2,0},{1,3},{3,1},{4,6},{6,4},{5,7},{7,5},{8,10},{10,8},{9,1... | collective-permute-start | bytes 983048 | tf_op jit(solution)/shard_map/ppermute | solution.py:540
  77.3 19.4 %collective-permute-start.26 = (bf16[128,1280]{1,0:T(8,128)(2,1)S(1)}, bf16[128,1280]{1,0:T(8,128)(2,1)S(1)}, u32[]{:S(2)}, u32[]{:S(2)}) collective-permute-start(bf16[128,1280]{1,0:T(8,128)(2,1)S(1)} %get-tuple-element.47), channel_id=1, source_target_pairs={{0,4},{4,0},{1,5},{5,1},{2,6},{6,2},{3,7},{7,3},{8,12},{12,8},{9,1... | collective-permute-start | bytes 983048 | tf_op jit(solution)/shard_map/ppermute | solution.py:540
  78.9 17.9 %collective-permute-start.27 = (bf16[128,1280]{1,0:T(8,128)(2,1)S(1)}, bf16[128,1280]{1,0:T(8,128)(2,1)S(1)}, u32[]{:S(2)}, u32[]{:S(2)}) collective-permute-start(bf16[128,1280]{1,0:T(8,128)(2,1)S(1)} %get-tuple-element.48), channel_id=1, source_target_pairs={{0,6},{2,4},{4,2},{6,0},{1,7},{3,5},{5,3},{7,1},{8,14},{10,12},{12... | collective-permute-start | bytes 983048 | tf_op jit(solution)/shard_map/ppermute | solution.py:658
  85.9 10.8 %collective-permute-start.31 = (bf16[160,512]{1,0:T(8,128)(2,1)S(1)}, bf16[160,512]{1,0:T(8,128)(2,1)S(1)}, u32[]{:S(2)}, u32[]{:S(2)}) collective-permute-start(bf16[160,512]{1,0:T(8,128)(2,1)S(1)} %get-tuple-element.53), channel_id=1, source_target_pairs={{0,2},{2,0},{1,3},{3,1},{4,6},{6,4},{5,7},{7,5},{8,10},{10,8},{9,1... | collective-permute-start | bytes 491528 | tf_op jit(solution)/shard_map/ppermute | solution.py:540
  86.9 11.7 %collective-permute-start.32 = (bf16[160,512]{1,0:T(8,128)(2,1)S(1)}, bf16[160,512]{1,0:T(8,128)(2,1)S(1)}, u32[]{:S(2)}, u32[]{:S(2)}) collective-permute-start(bf16[160,512]{1,0:T(8,128)(2,1)S(1)} %get-tuple-element.53), channel_id=1, source_target_pairs={{0,1},{1,0},{2,3},{3,2},{4,5},{5,4},{6,7},{7,6},{8,9},{9,8},{10,11... | collective-permute-start | bytes 491528 | tf_op jit(solution)/shard_map/ppermute | solution.py:540
  96.8 1.8 %collective-permute-start.33 = (bf16[160,512]{1,0:T(8,128)(2,1)S(1)}, bf16[160,512]{1,0:T(8,128)(2,1)}, u32[]{:S(2)}, u32[]{:S(2)}) collective-permute-start(bf16[160,512]{1,0:T(8,128)(2,1)S(1)} %collective-permute-done.31), channel_id=1, source_target_pairs={{0,1},{1,0},{2,3},{3,2},{4,5},{5,4},{6,7},{7,6},{8,9},{9,8},{10,11... | collective-permute-start | bytes 491528 | tf_op jit(solution)/shard_map/ppermute | solution.py:540
where the time goes:
time: 101 us; the launch traced here: 100 us
  starting transfers between devices  39.7 us (39%)
  waiting for transfers between devices  36 us (36%)
  Pallas kernels  18.6 us (18%)
  local copies, waits for them, and re-layouts  3.1 us (3%)
  other arithmetic  2.05 us (2%)
    ppermute x28, starting transfers between devices, shift(): return lax.ppermute(value, axis, pairs)  34.5 us
    ppermute x28, waiting for transfers between devices, shift(): return lax.ppermute(value, axis, pairs)  33.7 us
    pallas_call x1, Pallas kernels, attention_parts(): pl.pallas_call(functools.partial(attention_kernel, slots, half), grid_spe...  5.06 us
    ppermute x3, starting transfers between devices, step(): piece = lax.ppermute(piece, ('x', 'y'), pairs)  3.49 us
    pallas_call x1, Pallas kernels, row_products(): pl.pallas_call(functools.partial(row_kernel, z_size, groups), in_specs=[p...  3.22 us
    ppermute x3, waiting for transfers between devices, step(): piece = lax.ppermute(piece, ('x', 'y'), pairs)  2.3 us
    pallas_call x1, Pallas kernels, packed(): pl.pallas_call(functools.partial(pack_kernel, tok_rows), in_specs=[pl.Blo...  2.22 us
    pallas_call x2, Pallas kernels, sliced(): pl.pallas_call(kernel, in_specs=[pl.BlockSpec(memory_space=pltpu.SMEM)] +...  2.18 us
  transfers between devices with their start and end apart: 34, of which 12 were waited for; matrix products, arithmetic and copies ran while one was open for 2% of the time, Pallas kernels for 16%

commit v1 on v0

--- a/solution.py
+++ b/solution.py
@@ -211,22 +211,15 @@
 def owner_kernel(pieces, z_size, place, near, far, *refs):
     values, outs = refs[: 2 * pieces], refs[2 * pieces : 2 * pieces + z_size]
     token_rows = refs[2 * pieces + z_size]
-    buffers, totals, sems = refs[-3:]
-    copies = [
-        pltpu.make_async_copy(source, buffers.at[n], sems.at[n])
-        for n, source in enumerate((near, far))
-    ]
-    for copy in copies:
-        copy.start()
+    totals = refs[-1]
     sides = near.shape[0] // PAIR
     rows, tokens = near.shape[2:]
     half = values[0].shape[1]
-    for n, copy in enumerate(copies):
-        copy.wait()
+    for n, source in enumerate((near, far)):
         for m in range(PAIR):
             columns = jnp.concatenate(
                 [
-                    buffers[n, (x + m) % PAIR * sides + y].reshape(z_size * rows, tokens)
+                    source[(x + m) % PAIR * sides + y].reshape(z_size * rows, tokens)
                     for y in range(sides)
                     for x in range(PAIR)
                 ],
@@ -297,16 +290,12 @@
     shape = jax.ShapeDtypeStruct((rows, width), jnp.bfloat16)
     return pl.pallas_call(
         functools.partial(owner_kernel, pieces, z_size),
-        in_specs=[pl.BlockSpec(memory_space=pltpu.SMEM)]
-        + [pl.BlockSpec(memory_space=pl.ANY)] * 2
-        + [whole] * (2 * pieces),
+        in_specs=[pl.BlockSpec(memory_space=pltpu.SMEM)] + [whole] * (2 + 2 * pieces),
         out_specs=[whole] * (z_size + 1),
         out_shape=[shape] * z_size
         + [jax.ShapeDtypeStruct((near.shape[0] * tokens, width), jnp.bfloat16)],
         scratch_shapes=[
-            pltpu.VMEM((2, *near.shape), jnp.bfloat16),
             pltpu.VMEM((z_size * rows, width), jnp.float32),
-            pltpu.SemaphoreType.DMA((2,)),
         ],
         compiler_params=ROOM,
         cost_estimate=pl.CostEstimate(

time: 101 us -> 100 us (0.990)
  no operation moved by 1% of the time
where the time goes in v1:
time: 100 us
  starting transfers between devices  39.8 us (40%)
  waiting for transfers between devices  36 us (36%)
  Pallas kernels  18 us (18%)
  local copies, waits for them, and re-layouts  3.1 us (3%)
  other arithmetic  2.05 us (2%)
    ppermute x28, starting transfers between devices, shift(): return lax.ppermute(value, axis, pairs)  34.5 us
    ppermute x28, waiting for transfers between devices, shift(): return lax.ppermute(value, axis, pairs)  33.7 us
    pallas_call x1, Pallas kernels, attention_parts(): pl.pallas_call(functools.partial(attention_kernel, slots, half), grid_spe...  5.06 us
    ppermute x3, starting transfers between devices, step(): piece = lax.ppermute(piece, ('x', 'y'), pairs)  3.49 us
    pallas_call x1, Pallas kernels, row_products(): pl.pallas_call(functools.partial(row_kernel, z_size, groups), in_specs=[p...  3.21 us
    ppermute x3, waiting for transfers between devices, step(): piece = lax.ppermute(piece, ('x', 'y'), pairs)  2.3 us
    pallas_call x1, Pallas kernels, packed(): pl.pallas_call(functools.partial(pack_kernel, tok_rows), in_specs=[pl.Blo...  2.22 us
    pallas_call x2, Pallas kernels, sliced(): pl.pallas_call(kernel, in_specs=[pl.BlockSpec(memory_space=pltpu.SMEM)] +...  2.18 us
  transfers between devices with their start and end apart: 34, of which 12 were waited for; matrix products, arithmetic and copies ran while one was open for 2% of the time, Pallas kernels for 16%

profile of v1, /device:TPU:0, one launch (start us, length us, event | category | flops | bytes accessed | tf_op | source)
XLA Modules:
  0.0 100.0 jit_solution(10534307809883818355)
XLA Ops:
  0.7 2.2 %shard_map.149 = (bf16[256,256]{1,0:T(8,128)(2,1)}, bf16[128,256]{1,0:T(8,128)(2,1)}, bf16[128,1280]{1,0:T(8,128)(2,1)}, bf16[128,1280]{1,0:T(8,128)(2,1)}) custom-call(bf16[128,512]{1,0:T(8,128)(2,1)} %keys.1, bf16[128,2560]{1,0:T(8,128)(2,1)} %q_own.1, bf16[128,2560]{1,0:T(8,128)(2,1)} %g_own.1), custom_call_target="tpu_custom_call" | custom-call | bytes 1310720 | tf_op jit(solution)/shard_map/pallas_call | solution.py:194
  2.9 3.0 %collective-permute-start.7 = (bf16[128,256]{1,0:T(8,128)(2,1)}, bf16[128,256]{1,0:T(8,128)(2,1)S(1)}, u32[]{:S(2)}, u32[]{:S(2)}) collective-permute-start(bf16[128,256]{1,0:T(8,128)(2,1)} %get-tuple-element.39), channel_id=1, source_target_pairs={{0,4},{4,0},{1,5},{5,1},{2,6},{6,2},{3,7},{7,3},{8,12},{12,8},{9,1... | collective-permute-start | bytes 196616 | tf_op jit(solution)/shard_map/ppermute | solution.py:529
  6.1 2.7 %collective-permute-done.7 = bf16[128,256]{1,0:T(8,128)(2,1)S(1)} collective-permute-done((bf16[128,256]{1,0:T(8,128)(2,1)}, bf16[128,256]{1,0:T(8,128)(2,1)S(1)}, u32[]{:S(2)}, u32[]{:S(2)}) %collective-permute-start.7) | collective-permute-done | bytes 65568 | tf_op jit(solution)/shard_map/ppermute | solution.py:529
  8.8 0.6 constant_dynamic-update-slice_fusion.refs_0_
  9.4 4.3 %collective-permute-start.8 = (bf16[256,256]{1,0:T(8,128)(2,1)}, bf16[256,256]{1,0:T(8,128)(2,1)S(1)}, u32[]{:S(2)}, u32[]{:S(2)}) collective-permute-start(bf16[256,256]{1,0:T(8,128)(2,1)} %constant_dynamic-update-slice_fusion.refs_0_), channel_id=1, source_target_pairs={{0,8},{8,16},{16,24},{1,9},{9,17},{17,25},{2,10},{10,18},{18,26},{... | collective-permute-start | bytes 393224 | tf_op jit(solution)/shard_map/ppermute | solution.py:529
  13.7 4.5 %collective-permute-start.9 = (bf16[256,256]{1,0:T(8,128)(2,1)}, bf16[256,256]{1,0:T(8,128)(2,1)S(1)}, u32[]{:S(2)}, u32[]{:S(2)}) collective-permute-start(bf16[256,256]{1,0:T(8,128)(2,1)} %constant_dynamic-update-slice_fusion.refs_0_), channel_id=1, source_target_pairs={{0,16},{8,24},{1,17},{9,25},{2,18},{10,26},{3,19},{11,27},{4,20},{... | collective-permute-start | bytes 393224 | tf_op jit(solution)/shard_map/ppermute | solution.py:529
  18.2 1.9 %collective-permute-start.10 = (bf16[256,256]{1,0:T(8,128)(2,1)}, bf16[256,256]{1,0:T(8,128)(2,1)}, u32[]{:S(2)}, u32[]{:S(2)}) collective-permute-start(bf16[256,256]{1,0:T(8,128)(2,1)} %constant_dynamic-update-slice_fusion.refs_0_), channel_id=1, source_target_pairs={{0,24},{1,25},{2,26},{3,27},{4,28},{5,29},{6,30},{7,31}} | collective-permute-start | bytes 393224 | tf_op jit(solution)/shard_map/ppermute | solution.py:529
  20.3 0.6 shard_map.150.c_own
  20.9 1.6 %collective-permute-start.6 = (f32[1,128]{1,0:T(1,128)S(1)}, f32[1,128]{1,0:T(1,128)S(1)}, u32[]{:S(2)}, u32[]{:S(2)}) collective-permute-start(f32[1,128]{1,0:T(1,128)S(1)} %shard_map.150.c_own), channel_id=1, source_target_pairs={{0,4},{4,0},{1,5},{5,1},{2,6},{6,2},{3,7},{7,3},{8,12},{12,8},{9,1... | collective-permute-start | bytes 1544 | tf_op jit(solution)/shard_map/ppermute | solution.py:529
  22.5 2.0 %collective-permute-done.6.c_far = f32[1,128]{1,0:T(1,128)S(1)} collective-permute-done((f32[1,128]{1,0:T(1,128)S(1)}, f32[1,128]{1,0:T(1,128)S(1)}, u32[]{:S(2)}, u32[]{:S(2)}) %collective-permute-start.6) | collective-permute-done | bytes 544 | tf_op jit(solution)/shard_map/ppermute | solution.py:529
  24.5 1.6 %collective-permute-start.5 = (bf16[128,1280]{1,0:T(8,128)(2,1)}, bf16[128,1280]{1,0:T(8,128)(2,1)}, u32[]{:S(2)}, u32[]{:S(2)}) collective-permute-start(bf16[128,1280]{1,0:T(8,128)(2,1)} %get-tuple-element.37), channel_id=1, source_target_pairs={{0,4},{4,0},{1,5},{5,1},{2,6},{6,2},{3,7},{7,3},{8,12},{12,8},{9,1... | collective-permute-start | bytes 983048 | tf_op jit(solution)/shard_map/ppermute | solution.py:529
  26.1 0.8 copy.16
  26.9 1.6 %shard_map.147 = (bf16[4,2,160,128]{3,2,1,0:T(8,128)(2,1)S(1)}, bf16[4,2,160,128]{3,2,1,0:T(8,128)(2,1)}, bf16[4,2,160,128]{3,2,1,0:T(8,128)(2,1)}, bf16[4,2,160,128]{3,2,1,0:T(8,128)(2,1)}) custom-call(s32[4]{0:T(128)S(1)} %pad_add_fusion.place, bf16[4,2,2,2,160,128]{5,4,3,2,1,0:T(8,128)(2,1)S(1)} %bitcast.9), custom_call_target="tpu_custom_call" | custom-call | bytes 2621440 | tf_op jit(solution)/shard_map/pallas_call | solution.py:360
  28.5 0.7 copy-done.3
  29.2 1.5 %collective-permute-start = (bf16[4,2,160,128]{3,2,1,0:T(8,128)(2,1)}, bf16[4,2,160,128]{3,2,1,0:T(8,128)(2,1)S(1)}, u32[]{:S(2)}, u32[]{:S(2)}) collective-permute-start(bf16[4,2,160,128]{3,2,1,0:T(8,128)(2,1)} %get-tuple-element.31), channel_id=1, source_target_pairs={{0,2},{2,0},{4,6},{6,4},{1,3},{3,1},{5,7},{7,5},{8,10},{10,8},{12,... | collective-permute-start | bytes 983048 | tf_op jit(solution)/shard_map/ppermute | solution.py:597
  30.7 0.5 collective-permute-start.1
  31.2 1.5 %collective-permute-start.2 = (bf16[4,2,160,128]{3,2,1,0:T(8,128)(2,1)}, bf16[4,2,160,128]{3,2,1,0:T(8,128)(2,1)S(1)}, u32[]{:S(2)}, u32[]{:S(2)}) collective-permute-start(bf16[4,2,160,128]{3,2,1,0:T(8,128)(2,1)} %get-tuple-element.33), channel_id=1, source_target_pairs={{0,6},{2,4},{4,2},{6,0},{1,7},{3,5},{5,3},{7,1},{8,14},{10,12},{12... | collective-permute-start | bytes 983048 | tf_op jit(solution)/shard_map/ppermute | solution.py:597
  32.8 1.7 %collective-permute-done.5.g_far = bf16[128,1280]{1,0:T(8,128)(2,1)} collective-permute-done((bf16[128,1280]{1,0:T(8,128)(2,1)}, bf16[128,1280]{1,0:T(8,128)(2,1)}, u32[]{:S(2)}, u32[]{:S(2)}) %collective-permute-start.5) | collective-permute-done | bytes 327712 | tf_op jit(solution)/shard_map/ppermute | solution.py:529
  34.5 0.9 copy-done.12
  35.4 5.1 %shard_map.151 = (bf16[256,256]{1,0:T(8,128)(2,1)S(1)}, bf16[256,256]{1,0:T(8,128)(2,1)S(1)}, bf16[256,256]{1,0:T(8,128)(2,1)S(1)}, bf16[256,256]{1,0:T(8,128)(2,1)S(1)}) custom-call(s32[4]{0:T(128)S(1)} %pad_add_fusion.place, bf16[128,2560]{1,0:T(8,128)(2,1)S(1)} %copy-done.1, bf16[128,1280]{1,0:T(8,128)(2,1)} %collective-permute-done.4.q_far, ...), custom_call_target="tpu_custom_call" | custom-call | flops 671088640 | bytes 1310720 | tf_op jit(solution)/shard_map/pallas_call | solution.py:143
  40.5 1.3 %collective-permute-start.13 = (bf16[256,256]{1,0:T(8,128)(2,1)S(1)}, bf16[256,256]{1,0:T(8,128)(2,1)S(1)}, u32[]{:S(2)}, u32[]{:S(2)}) collective-permute-start(bf16[256,256]{1,0:T(8,128)(2,1)S(1)} %get-tuple-element.43), channel_id=1, source_target_pairs={{24,0},{25,1},{26,2},{27,3},{28,4},{29,5},{30,6},{31,7}} | collective-permute-start | bytes 393224 | tf_op jit(solution)/shard_map/ppermute | solution.py:529
  41.8 1.3 %collective-permute-start.12 = (bf16[256,256]{1,0:T(8,128)(2,1)S(1)}, bf16[256,256]{1,0:T(8,128)(2,1)S(1)}, u32[]{:S(2)}, u32[]{:S(2)}) collective-permute-start(bf16[256,256]{1,0:T(8,128)(2,1)S(1)} %get-tuple-element.42), channel_id=1, source_target_pairs={{16,0},{24,8},{17,1},{25,9},{18,2},{26,10},{19,3},{27,11},{20,4},{... | collective-permute-start | bytes 393224 | tf_op jit(solution)/shard_map/ppermute | solution.py:529
  43.1 1.3 %collective-permute-start.11 = (bf16[256,256]{1,0:T(8,128)(2,1)S(1)}, bf16[256,256]{1,0:T(8,128)(2,1)S(1)}, u32[]{:S(2)}, u32[]{:S(2)}) collective-permute-start(bf16[256,256]{1,0:T(8,128)(2,1)S(1)} %get-tuple-element.41), channel_id=1, source_target_pairs={{8,0},{16,8},{24,16},{9,1},{17,9},{25,17},{10,2},{18,10},{26,18},{... | collective-permute-start | bytes 393224 | tf_op jit(solution)/shard_map/ppermute | solution.py:529
  44.4 2.3 %collective-permute-done.2.refs_3_ = bf16[4,2,160,128]{3,2,1,0:T(8,128)(2,1)S(1)} collective-permute-done((bf16[4,2,160,128]{3,2,1,0:T(8,128)(2,1)}, bf16[4,2,160,128]{3,2,1,0:T(8,128)(2,1)S(1)}, u32[]{:S(2)}, u32[]{:S(2)}) %collective-permute-start.2) | collective-permute-done | bytes 327712 | tf_op jit(solution)/shard_map/ppermute | solution.py:597
  46.7 0.6 shard_map.148
  47.5 0.4 collective-permute-start.22
  47.9 1.4 %collective-permute-done.13 = bf16[256,256]{1,0:T(8,128)(2,1)S(1)} collective-permute-done((bf16[256,256]{1,0:T(8,128)(2,1)S(1)}, bf16[256,256]{1,0:T(8,128)(2,1)S(1)}, u32[]{:S(2)}, u32[]{:S(2)}) %collective-permute-start.13) | collective-permute-done | bytes 131104 | tf_op jit(solution)/shard_map/ppermute | solution.py:529
  49.3 2.7 %collective-permute-done.12 = bf16[256,256]{1,0:T(8,128)(2,1)S(1)} collective-permute-done((bf16[256,256]{1,0:T(8,128)(2,1)S(1)}, bf16[256,256]{1,0:T(8,128)(2,1)S(1)}, u32[]{:S(2)}, u32[]{:S(2)}) %collective-permute-start.12) | collective-permute-done | bytes 131104 | tf_op jit(solution)/shard_map/ppermute | solution.py:529
  52.1 3.7 %collective-permute-start.14 = (bf16[256,256]{1,0:T(8,128)(2,1)S(1)}, bf16[256,256]{1,0:T(8,128)(2,1)S(1)}, u32[]{:S(2)}, u32[]{:S(2)}) collective-permute-start(bf16[256,256]{1,0:T(8,128)(2,1)S(1)} %add_convert_fusion.refs_0_), channel_id=1, source_target_pairs={{0,2},{2,0},{1,3},{3,1},{4,6},{6,4},{5,7},{7,5},{8,10},{10,8},{9,1... | collective-permute-start | bytes 393224 | tf_op jit(solution)/shard_map/ppermute | solution.py:529
  55.9 1.6 %collective-permute-start.17 = (bf16[256,256]{1,0:T(8,128)(2,1)S(1)}, bf16[256,256]{1,0:T(8,128)(2,1)S(1)}, u32[]{:S(2)}, u32[]{:S(2)}) collective-permute-start(bf16[256,256]{1,0:T(8,128)(2,1)S(1)} %add_convert_fusion.refs_0_), channel_id=1, source_target_pairs={{0,4},{4,0},{1,5},{5,1},{2,6},{6,2},{3,7},{7,3},{8,12},{12,8},{9,1... | collective-permute-start | bytes 393224 | tf_op jit(solution)/shard_map/ppermute | solution.py:529
  57.4 1.4 %collective-permute-done.14.refs_1_ = bf16[256,256]{1,0:T(8,128)(2,1)S(1)} collective-permute-done((bf16[256,256]{1,0:T(8,128)(2,1)S(1)}, bf16[256,256]{1,0:T(8,128)(2,1)S(1)}, u32[]{:S(2)}, u32[]{:S(2)}) %collective-permute-start.14) | collective-permute-done | bytes 131104 | tf_op jit(solution)/shard_map/ppermute | solution.py:529
  58.8 2.0 %collective-permute-done.17.refs_4_ = bf16[256,256]{1,0:T(8,128)(2,1)S(1)} collective-permute-done((bf16[256,256]{1,0:T(8,128)(2,1)S(1)}, bf16[256,256]{1,0:T(8,128)(2,1)S(1)}, u32[]{:S(2)}, u32[]{:S(2)}) %collective-permute-start.17) | collective-permute-done | bytes 131104 | tf_op jit(solution)/shard_map/ppermute | solution.py:529
  61.6 4.2 %collective-permute-done.18.refs_5_ = bf16[256,256]{1,0:T(8,128)(2,1)S(1)} collective-permute-done((bf16[256,256]{1,0:T(8,128)(2,1)S(1)}, bf16[256,256]{1,0:T(8,128)(2,1)S(1)}, u32[]{:S(2)}, u32[]{:S(2)}) %collective-permute-start.18) | collective-permute-done | bytes 131104 | tf_op jit(solution)/shard_map/ppermute | solution.py:529
  65.8 1.3 %collective-permute-done.20.refs_7_ = bf16[256,256]{1,0:T(8,128)(2,1)S(1)} collective-permute-done((bf16[256,256]{1,0:T(8,128)(2,1)S(1)}, bf16[256,256]{1,0:T(8,128)(2,1)S(1)}, u32[]{:S(2)}, u32[]{:S(2)}) %collective-permute-start.20) | collective-permute-done | bytes 131104 | tf_op jit(solution)/shard_map/ppermute | solution.py:529
  67.2 1.5 %shard_map.152 = (bf16[160,512]{1,0:T(8,128)(2,1)S(1)}, bf16[160,512]{1,0:T(8,128)(2,1)S(1)}, bf16[160,512]{1,0:T(8,128)(2,1)S(1)}, bf16[160,512]{1,0:T(8,128)(2,1)S(1)}, bf16[512,512]{1,0:T(8,128)(2,1)S(1)}) custom-call(s32[4]{0:T(128)S(1)} %pad_add_fusion.place, bf16[4,4,160,128]{3,2,1,0:T(8,128)(2,1)S(1)} %get-tuple-element.34.near, ...), custom_call_target="tpu_custom_call" | custom-call | flops 671088640 | bytes 2621440 | tf_op jit(solution)/shard_map/pallas_call | solution.py:291
  68.7 0.7 collective-permute-start.28
  69.7 2.8 %collective-permute-start.30 = (bf16[160,512]{1,0:T(8,128)(2,1)S(1)}, bf16[160,512]{1,0:T(8,128)(2,1)S(1)}, u32[]{:S(2)}, u32[]{:S(2)}) collective-permute-start(bf16[160,512]{1,0:T(8,128)(2,1)S(1)} %get-tuple-element.52), channel_id=1, source_target_pairs={{0,24},{8,0},{16,8},{24,16},{1,25},{9,1},{17,9},{25,17},{2,26},{10... | collective-permute-start | bytes 491528 | tf_op jit(solution)/shard_map/ppermute | solution.py:529
  72.6 3.2 %shard_map.153 = (bf16[128,1280]{1,0:T(8,128)(2,1)S(1)}, bf16[128,1280]{1,0:T(8,128)(2,1)S(1)}, bf16[128,1280]{1,0:T(8,128)(2,1)S(1)}, bf16[128,1280]{1,0:T(8,128)(2,1)S(1)}) custom-call(s32[4]{0:T(128)S(1)} %pad_add_fusion.place, bf16[512,512]{1,0:T(8,128)(2,1)S(1)} %get-tuple-element.44.token_rows, bf16[2,160,512]{2,1,0:T(8,128)(2,1)S(1)} %pad_maximum_fusion.1.refs_0_, ...), custom_call_target="tpu_custom_call" | custom-call | flops 671088640 | bytes 2621440 | tf_op jit(solution)/shard_map/pallas_call | solution.py:404
  75.8 1.0 %collective-permute-start.25 = (bf16[128,1280]{1,0:T(8,128)(2,1)S(1)}, bf16[128,1280]{1,0:T(8,128)(2,1)S(1)}, u32[]{:S(2)}, u32[]{:S(2)}) collective-permute-start(bf16[128,1280]{1,0:T(8,128)(2,1)S(1)} %get-tuple-element.46), channel_id=1, source_target_pairs={{0,2},{2,0},{1,3},{3,1},{4,6},{6,4},{5,7},{7,5},{8,10},{10,8},{9,1... | collective-permute-start | bytes 983048 | tf_op jit(solution)/shard_map/ppermute | solution.py:529
  76.8 1.6 %collective-permute-start.26 = (bf16[128,1280]{1,0:T(8,128)(2,1)S(1)}, bf16[128,1280]{1,0:T(8,128)(2,1)S(1)}, u32[]{:S(2)}, u32[]{:S(2)}) collective-permute-start(bf16[128,1280]{1,0:T(8,128)(2,1)S(1)} %get-tuple-element.47), channel_id=1, source_target_pairs={{0,4},{4,0},{1,5},{5,1},{2,6},{6,2},{3,7},{7,3},{8,12},{12,8},{9,1... | collective-permute-start | bytes 983048 | tf_op jit(solution)/shard_map/ppermute | solution.py:529
  78.4 1.3 %collective-permute-start.27 = (bf16[128,1280]{1,0:T(8,128)(2,1)S(1)}, bf16[128,1280]{1,0:T(8,128)(2,1)S(1)}, u32[]{:S(2)}, u32[]{:S(2)}) collective-permute-start(bf16[128,1280]{1,0:T(8,128)(2,1)S(1)} %get-tuple-element.48), channel_id=1, source_target_pairs={{0,6},{2,4},{4,2},{6,0},{1,7},{3,5},{5,3},{7,1},{8,14},{10,12},{12... | collective-permute-start | bytes 983048 | tf_op jit(solution)/shard_map/ppermute | solution.py:647
  79.7 4.2 %collective-permute-done.29.refs_2_ = bf16[160,512]{1,0:T(8,128)(2,1)S(1)} collective-permute-done((bf16[160,512]{1,0:T(8,128)(2,1)S(1)}, bf16[160,512]{1,0:T(8,128)(2,1)S(1)}, u32[]{:S(2)}, u32[]{:S(2)}) %collective-permute-start.29) | collective-permute-done | bytes 163872 | tf_op jit(solution)/shard_map/ppermute | solution.py:529
  83.9 1.5 %shard_map.155 = (bf16[160,512]{1,0:T(8,128)(2,1)S(1)}, bf16[160,512]{1,0:T(8,128)(2,1)}, bf16[160,512]{1,0:T(8,128)(2,1)}) custom-call(s32[4]{0:T(128)S(1)} %pad_add_fusion.place, bf16[160,512]{1,0:T(8,128)(2,1)S(1)} %get-tuple-element.49.refs_0_, bf16[160,512]{1,0:T(8,128)(2,1)S(1)} %collective-permute-done.28.refs_1_, ...), custom_call_target="tpu_custom_call" | custom-call | flops 3276800 | bytes 1638400 | tf_op jit(solution)/shard_map/pallas_call | solution.py:512
  85.4 0.9 collective-permute-start.31
  86.4 9.9 %collective-permute-done.31 = bf16[160,512]{1,0:T(8,128)(2,1)S(1)} collective-permute-done((bf16[160,512]{1,0:T(8,128)(2,1)S(1)}, bf16[160,512]{1,0:T(8,128)(2,1)S(1)}, u32[]{:S(2)}, u32[]{:S(2)}) %collective-permute-start.31) | collective-permute-done | bytes 163872 | tf_op jit(solution)/shard_map/ppermute | solution.py:529
  96.3 1.8 %shard_map.154 = bf16[128,5120]{1,0:T(8,128)(2,1)} custom-call(s32[4]{0:T(128)S(1)} %pad_add_fusion.place, bf16[128,1280]{1,0:T(8,128)(2,1)S(1)} %get-tuple-element.45.refs_0_, bf16[128,1280]{1,0:T(8,128)(2,1)S(1)} %collective-permute-done.25.refs_1_, bf16[128,1280]{1,0:T(8,128)(2,1)S(1)} %collective-permute-done.26.refs_2_, ...), custom_call_target="tpu_custom_call" | custom-call | bytes 2621440 | tf_op jit(solution)/shard_map/pallas_call | solution.py:462
  98.1 1.0 broadcast_select_fusion.7
  99.1 0.9 pad_maximum_fusion
  (65 shorter events, 1.6 us)
Async XLA Ops:
  0.6 32.0 %copy-start = (bf16[640,512]{1,0:T(8,128)(2,1)S(1)}, bf16[640,512]{1,0:T(8,128)(2,1)}, u32[]{:S(2)}) copy-start(bf16[640,512]{1,0:T(8,128)(2,1)} %param.21) | copy-start | bytes 1966084
  0.6 19.6 %copy-start.7 = (f32[8]{0:T(128)S(1)}, f32[8]{0:T(128)}, u32[]{:S(2)}) copy-start(f32[8]{0:T(128)} %rewards.1) | copy-start | bytes 100
  0.7 19.6 %copy-start.8 = (s32[8]{0:T(128)S(1)}, s32[8]{0:T(128)}, u32[]{:S(2)}) copy-start(s32[8]{0:T(128)} %group_ids.1) | copy-start | bytes 100
  0.7 19.6 %copy-start.9 = (s32[8]{0:T(128)S(1)}, s32[8]{0:T(128)}, u32[]{:S(2)}) copy-start(s32[8]{0:T(128)} %lengths.1) | copy-start | bytes 100
  0.7 19.6 %copy-start.10 = (f32[128]{0:T(128)S(1)}, f32[128]{0:T(128)}, u32[]{:S(2)}) copy-start(f32[128]{0:T(128)} %param.16) | copy-start | bytes 1540
  0.7 19.6 %copy-start.11 = (f32[128]{0:T(128)S(1)}, f32[128]{0:T(128)}, u32[]{:S(2)}) copy-start(f32[128]{0:T(128)} %param.17) | copy-start | bytes 1540
  0.7 25.4 %copy-start.13 = (bf16[128,5120]{1,0:T(8,128)(2,1)S(1)}, bf16[128,5120]{1,0:T(8,128)(2,1)}, u32[]{:S(2)}) copy-start(bf16[128,5120]{1,0:T(8,128)(2,1)} %param.12) | copy-start | bytes 3932164
  2.9 5.8 %collective-permute-start.7 = (bf16[128,256]{1,0:T(8,128)(2,1)}, bf16[128,256]{1,0:T(8,128)(2,1)S(1)}, u32[]{:S(2)}, u32[]{:S(2)}) collective-permute-start(bf16[128,256]{1,0:T(8,128)(2,1)} %get-tuple-element.39), channel_id=1, source_target_pairs={{0,4},{4,0},{1,5},{5,1},{2,6},{6,2},{3,7},{7,3},{8,12},{12,8},{9,1... | collective-permute-start | bytes 196616 | tf_op jit(solution)/shard_map/ppermute | solution.py:529
  6.0 26.7 %collective-permute-start.4 = (bf16[128,1280]{1,0:T(8,128)(2,1)}, bf16[128,1280]{1,0:T(8,128)(2,1)}, u32[]{:S(2)}, u32[]{:S(2)}) collective-permute-start(bf16[128,1280]{1,0:T(8,128)(2,1)} %get-tuple-element.36), channel_id=1, source_target_pairs={{0,4},{4,0},{1,5},{5,1},{2,6},{6,2},{3,7},{7,3},{8,12},{12,8},{9,1... | collective-permute-start | bytes 983048 | tf_op jit(solution)/shard_map/ppermute | solution.py:529
  9.4 19.8 %collective-permute-start.8 = (bf16[256,256]{1,0:T(8,128)(2,1)}, bf16[256,256]{1,0:T(8,128)(2,1)S(1)}, u32[]{:S(2)}, u32[]{:S(2)}) collective-permute-start(bf16[256,256]{1,0:T(8,128)(2,1)} %constant_dynamic-update-slice_fusion.refs_0_), channel_id=1, source_target_pairs={{0,8},{8,16},{16,24},{1,9},{9,17},{17,25},{2,10},{10,18},{18,26},{... | collective-permute-start | bytes 393224 | tf_op jit(solution)/shard_map/ppermute | solution.py:529
  13.7 17.0 %collective-permute-start.9 = (bf16[256,256]{1,0:T(8,128)(2,1)}, bf16[256,256]{1,0:T(8,128)(2,1)S(1)}, u32[]{:S(2)}, u32[]{:S(2)}) collective-permute-start(bf16[256,256]{1,0:T(8,128)(2,1)} %constant_dynamic-update-slice_fusion.refs_0_), channel_id=1, source_target_pairs={{0,16},{8,24},{1,17},{9,25},{2,18},{10,26},{3,19},{11,27},{4,20},{... | collective-permute-start | bytes 393224 | tf_op jit(solution)/shard_map/ppermute | solution.py:529
  18.2 13.0 %collective-permute-start.10 = (bf16[256,256]{1,0:T(8,128)(2,1)}, bf16[256,256]{1,0:T(8,128)(2,1)}, u32[]{:S(2)}, u32[]{:S(2)}) collective-permute-start(bf16[256,256]{1,0:T(8,128)(2,1)} %constant_dynamic-update-slice_fusion.refs_0_), channel_id=1, source_target_pairs={{0,24},{1,25},{2,26},{3,27},{4,28},{5,29},{6,30},{7,31}} | collective-permute-start | bytes 393224 | tf_op jit(solution)/shard_map/ppermute | solution.py:529
  20.9 3.6 %collective-permute-start.6 = (f32[1,128]{1,0:T(1,128)S(1)}, f32[1,128]{1,0:T(1,128)S(1)}, u32[]{:S(2)}, u32[]{:S(2)}) collective-permute-start(f32[1,128]{1,0:T(1,128)S(1)} %shard_map.150.c_own), channel_id=1, source_target_pairs={{0,4},{4,0},{1,5},{5,1},{2,6},{6,2},{3,7},{7,3},{8,12},{12,8},{9,1... | collective-permute-start | bytes 1544 | tf_op jit(solution)/shard_map/ppermute | solution.py:529
  24.5 10.0 %collective-permute-start.5 = (bf16[128,1280]{1,0:T(8,128)(2,1)}, bf16[128,1280]{1,0:T(8,128)(2,1)}, u32[]{:S(2)}, u32[]{:S(2)}) collective-permute-start(bf16[128,1280]{1,0:T(8,128)(2,1)} %get-tuple-element.37), channel_id=1, source_target_pairs={{0,4},{4,0},{1,5},{5,1},{2,6},{6,2},{3,7},{7,3},{8,12},{12,8},{9,1... | collective-permute-start | bytes 983048 | tf_op jit(solution)/shard_map/ppermute | solution.py:529
  26.9 7.6 %copy-start.1 = (bf16[128,2560]{1,0:T(8,128)(2,1)S(1)}, bf16[128,2560]{1,0:T(8,128)(2,1)}, u32[]{:S(2)}) copy-start(bf16[128,2560]{1,0:T(8,128)(2,1)} %q_own.1) | copy-start | bytes 1966084
  26.9 7.6 %copy-start.2 = (bf16[128,2560]{1,0:T(8,128)(2,1)S(1)}, bf16[128,2560]{1,0:T(8,128)(2,1)}, u32[]{:S(2)}) copy-start(bf16[128,2560]{1,0:T(8,128)(2,1)} %g_own.1) | copy-start | bytes 1966084
  28.5 0.7 copy-start.3
  29.2 12.6 %collective-permute-start = (bf16[4,2,160,128]{3,2,1,0:T(8,128)(2,1)}, bf16[4,2,160,128]{3,2,1,0:T(8,128)(2,1)S(1)}, u32[]{:S(2)}, u32[]{:S(2)}) collective-permute-start(bf16[4,2,160,128]{3,2,1,0:T(8,128)(2,1)} %get-tuple-element.31), channel_id=1, source_target_pairs={{0,2},{2,0},{4,6},{6,4},{1,3},{3,1},{5,7},{7,5},{8,10},{10,8},{12,... | collective-permute-start | bytes 983048 | tf_op jit(solution)/shard_map/ppermute | solution.py:597
  30.7 12.4 %collective-permute-start.1 = (bf16[4,2,160,128]{3,2,1,0:T(8,128)(2,1)}, bf16[4,2,160,128]{3,2,1,0:T(8,128)(2,1)S(1)}, u32[]{:S(2)}, u32[]{:S(2)}) collective-permute-start(bf16[4,2,160,128]{3,2,1,0:T(8,128)(2,1)} %get-tuple-element.32), channel_id=1, source_target_pairs={{0,4},{2,6},{4,0},{6,2},{1,5},{3,7},{5,1},{7,3},{8,12},{10,14},{12... | collective-permute-start | bytes 983048 | tf_op jit(solution)/shard_map/ppermute | solution.py:597
  31.2 15.5 %collective-permute-start.2 = (bf16[4,2,160,128]{3,2,1,0:T(8,128)(2,1)}, bf16[4,2,160,128]{3,2,1,0:T(8,128)(2,1)S(1)}, u32[]{:S(2)}, u32[]{:S(2)}) collective-permute-start(bf16[4,2,160,128]{3,2,1,0:T(8,128)(2,1)} %get-tuple-element.33), channel_id=1, source_target_pairs={{0,6},{2,4},{4,2},{6,0},{1,7},{3,5},{5,3},{7,1},{8,14},{10,12},{12... | collective-permute-start | bytes 983048 | tf_op jit(solution)/shard_map/ppermute | solution.py:597
  32.7 14.0 %copy-start.4 = (bf16[4,2,160,128]{3,2,1,0:T(8,128)(2,1)S(1)}, bf16[4,2,160,128]{3,2,1,0:T(8,128)(2,1)}, u32[]{:S(2)}) copy-start(bf16[4,2,160,128]{3,2,1,0:T(8,128)(2,1)} %copy-done.3) | copy-start | bytes 983044
  32.7 14.7 %collective-permute-start.21 = (bf16[1,160,512]{2,1,0:T(8,128)(2,1)S(1)}, bf16[1,160,512]{2,1,0:T(8,128)(2,1)S(1)}, u32[]{:S(2)}, u32[]{:S(2)}) collective-permute-start(bf16[1,160,512]{2,1,0:T(8,128)(2,1)S(1)} %bitcast.10), channel_id=1, source_target_pairs={{0,16},{8,24},{16,0},{24,8},{1,17},{9,25},{17,1},{25,9},{2,18},{10... | collective-permute-start | bytes 491528 | tf_op jit(solution)/shard_map/ppermute | solution.py:614
  34.5 0.9 copy-start.12
  40.5 8.8 %collective-permute-start.13 = (bf16[256,256]{1,0:T(8,128)(2,1)S(1)}, bf16[256,256]{1,0:T(8,128)(2,1)S(1)}, u32[]{:S(2)}, u32[]{:S(2)}) collective-permute-start(bf16[256,256]{1,0:T(8,128)(2,1)S(1)} %get-tuple-element.43), channel_id=1, source_target_pairs={{24,0},{25,1},{26,2},{27,3},{28,4},{29,5},{30,6},{31,7}} | collective-permute-start | bytes 393224 | tf_op jit(solution)/shard_map/ppermute | solution.py:529
  41.8 10.3 %collective-permute-start.12 = (bf16[256,256]{1,0:T(8,128)(2,1)S(1)}, bf16[256,256]{1,0:T(8,128)(2,1)S(1)}, u32[]{:S(2)}, u32[]{:S(2)}) collective-permute-start(bf16[256,256]{1,0:T(8,128)(2,1)S(1)} %get-tuple-element.42), channel_id=1, source_target_pairs={{16,0},{24,8},{17,1},{25,9},{18,2},{26,10},{19,3},{27,11},{20,4},{... | collective-permute-start | bytes 393224 | tf_op jit(solution)/shard_map/ppermute | solution.py:529
  43.1 8.9 %collective-permute-start.11 = (bf16[256,256]{1,0:T(8,128)(2,1)S(1)}, bf16[256,256]{1,0:T(8,128)(2,1)S(1)}, u32[]{:S(2)}, u32[]{:S(2)}) collective-permute-start(bf16[256,256]{1,0:T(8,128)(2,1)S(1)} %get-tuple-element.41), channel_id=1, source_target_pairs={{8,0},{16,8},{24,16},{9,1},{17,9},{25,17},{10,2},{18,10},{26,18},{... | collective-permute-start | bytes 393224 | tf_op jit(solution)/shard_map/ppermute | solution.py:529
  47.4 19.8 %collective-permute-start.3 = (bf16[4,4,160,128]{3,2,1,0:T(8,128)(2,1)S(1)}, bf16[4,4,160,128]{3,2,1,0:T(8,128)(2,1)S(1)}, u32[]{:S(2)}, u32[]{:S(2)}) collective-permute-start(bf16[4,4,160,128]{3,2,1,0:T(8,128)(2,1)S(1)} %get-tuple-element.35), channel_id=1, source_target_pairs={{0,1},{1,0},{2,3},{3,2},{4,5},{5,4},{6,7},{7,6},{8,9},{9,8},{10,11... | collective-permute-start | bytes 1966088 | tf_op jit(solution)/shard_map/ppermute | solution.py:529
  47.5 13.4 %collective-permute-start.22 = (bf16[2,160,512]{2,1,0:T(8,128)(2,1)S(1)}, bf16[2,160,512]{2,1,0:T(8,128)(2,1)S(1)}, u32[]{:S(2)}, u32[]{:S(2)}) collective-permute-start(bf16[2,160,512]{2,1,0:T(8,128)(2,1)S(1)} %pad_maximum_fusion.1.refs_0_), channel_id=1, source_target_pairs={{0,8},{8,0},{16,24},{24,16},{1,9},{9,1},{17,25},{25,17},{2,10},{10... | collective-permute-start | bytes 983048 | tf_op jit(solution)/shard_map/ppermute | solution.py:614
  52.1 6.7 %collective-permute-start.14 = (bf16[256,256]{1,0:T(8,128)(2,1)S(1)}, bf16[256,256]{1,0:T(8,128)(2,1)S(1)}, u32[]{:S(2)}, u32[]{:S(2)}) collective-permute-start(bf16[256,256]{1,0:T(8,128)(2,1)S(1)} %add_convert_fusion.refs_0_), channel_id=1, source_target_pairs={{0,2},{2,0},{1,3},{3,1},{4,6},{6,4},{5,7},{7,5},{8,10},{10,8},{9,1... | collective-permute-start | bytes 393224 | tf_op jit(solution)/shard_map/ppermute | solution.py:529
  55.9 5.0 %collective-permute-start.17 = (bf16[256,256]{1,0:T(8,128)(2,1)S(1)}, bf16[256,256]{1,0:T(8,128)(2,1)S(1)}, u32[]{:S(2)}, u32[]{:S(2)}) collective-permute-start(bf16[256,256]{1,0:T(8,128)(2,1)S(1)} %add_convert_fusion.refs_0_), channel_id=1, source_target_pairs={{0,4},{4,0},{1,5},{5,1},{2,6},{6,2},{3,7},{7,3},{8,12},{12,8},{9,1... | collective-permute-start | bytes 393224 | tf_op jit(solution)/shard_map/ppermute | solution.py:529
  57.4 3.6 %collective-permute-start.15 = (bf16[256,256]{1,0:T(8,128)(2,1)S(1)}, bf16[256,256]{1,0:T(8,128)(2,1)S(1)}, u32[]{:S(2)}, u32[]{:S(2)}) collective-permute-start(bf16[256,256]{1,0:T(8,128)(2,1)S(1)} %add_convert_fusion.refs_0_), channel_id=1, source_target_pairs={{0,1},{1,0},{2,3},{3,2},{4,5},{5,4},{6,7},{7,6},{8,9},{9,8},{10,11... | collective-permute-start | bytes 393224 | tf_op jit(solution)/shard_map/ppermute | solution.py:529
  58.8 2.6 %collective-permute-start.16 = (bf16[256,256]{1,0:T(8,128)(2,1)S(1)}, bf16[256,256]{1,0:T(8,128)(2,1)S(1)}, u32[]{:S(2)}, u32[]{:S(2)}) collective-permute-start(bf16[256,256]{1,0:T(8,128)(2,1)S(1)} %collective-permute-done.14.refs_1_), channel_id=1, source_target_pairs={{0,1},{1,0},{2,3},{3,2},{4,5},{5,4},{6,7},{7,6},{8,9},{9,8},{10,11... | collective-permute-start | bytes 393224 | tf_op jit(solution)/shard_map/ppermute | solution.py:529
  60.8 5.0 %collective-permute-start.18 = (bf16[256,256]{1,0:T(8,128)(2,1)S(1)}, bf16[256,256]{1,0:T(8,128)(2,1)S(1)}, u32[]{:S(2)}, u32[]{:S(2)}) collective-permute-start(bf16[256,256]{1,0:T(8,128)(2,1)S(1)} %collective-permute-done.17.refs_4_), channel_id=1, source_target_pairs={{0,2},{2,0},{1,3},{3,1},{4,6},{6,4},{5,7},{7,5},{8,10},{10,8},{9,1... | collective-permute-start | bytes 393224 | tf_op jit(solution)/shard_map/ppermute | solution.py:529
  60.9 11.7 %collective-permute-start.23 = (bf16[2,160,512]{2,1,0:T(8,128)(2,1)S(1)}, bf16[2,160,512]{2,1,0:T(8,128)(2,1)S(1)}, u32[]{:S(2)}, u32[]{:S(2)}) collective-permute-start(bf16[2,160,512]{2,1,0:T(8,128)(2,1)S(1)} %pad_maximum_fusion.1.refs_0_), channel_id=1, source_target_pairs={{0,1},{1,0},{2,3},{3,2},{4,5},{5,4},{6,7},{7,6},{8,9},{9,8},{10,11... | collective-permute-start | bytes 983048 | tf_op jit(solution)/shard_map/ppermute | solution.py:529
  61.1 11.5 %collective-permute-start.24 = (bf16[2,160,512]{2,1,0:T(8,128)(2,1)S(1)}, bf16[2,160,512]{2,1,0:T(8,128)(2,1)S(1)}, u32[]{:S(2)}, u32[]{:S(2)}) collective-permute-start(bf16[2,160,512]{2,1,0:T(8,128)(2,1)S(1)} %collective-permute-done.22.refs_1_), channel_id=1, source_target_pairs={{0,1},{1,0},{2,3},{3,2},{4,5},{5,4},{6,7},{7,6},{8,9},{9,8},{10,11... | collective-permute-start | bytes 983048 | tf_op jit(solution)/shard_map/ppermute | solution.py:529
  61.4 4.4 %collective-permute-start.19 = (bf16[256,256]{1,0:T(8,128)(2,1)S(1)}, bf16[256,256]{1,0:T(8,128)(2,1)S(1)}, u32[]{:S(2)}, u32[]{:S(2)}) collective-permute-start(bf16[256,256]{1,0:T(8,128)(2,1)S(1)} %collective-permute-done.17.refs_4_), channel_id=1, source_target_pairs={{0,1},{1,0},{2,3},{3,2},{4,5},{5,4},{6,7},{7,6},{8,9},{9,8},{10,11... | collective-permute-start | bytes 393224 | tf_op jit(solution)/shard_map/ppermute | solution.py:529
  65.8 1.3 %collective-permute-start.20 = (bf16[256,256]{1,0:T(8,128)(2,1)S(1)}, bf16[256,256]{1,0:T(8,128)(2,1)S(1)}, u32[]{:S(2)}, u32[]{:S(2)}) collective-permute-start(bf16[256,256]{1,0:T(8,128)(2,1)S(1)} %collective-permute-done.18.refs_5_), channel_id=1, source_target_pairs={{0,1},{1,0},{2,3},{3,2},{4,5},{5,4},{6,7},{7,6},{8,9},{9,8},{10,11... | collective-permute-start | bytes 393224 | tf_op jit(solution)/shard_map/ppermute | solution.py:529
  68.6 15.3 %copy-start.5 = (bf16[160,512]{1,0:T(8,128)(2,1)S(1)}, bf16[160,512]{1,0:T(8,128)(2,1)}, u32[]{:S(2)}) copy-start(bf16[160,512]{1,0:T(8,128)(2,1)} %refs_5_.1) | copy-start | bytes 491524
  68.7 15.3 %copy-start.6 = (bf16[160,512]{1,0:T(8,128)(2,1)S(1)}, bf16[160,512]{1,0:T(8,128)(2,1)}, u32[]{:S(2)}) copy-start(bf16[160,512]{1,0:T(8,128)(2,1)} %refs_6_.1) | copy-start | bytes 491524
  68.7 9.7 %collective-permute-start.28 = (bf16[160,512]{1,0:T(8,128)(2,1)S(1)}, bf16[160,512]{1,0:T(8,128)(2,1)S(1)}, u32[]{:S(2)}, u32[]{:S(2)}) collective-permute-start(bf16[160,512]{1,0:T(8,128)(2,1)S(1)} %get-tuple-element.50), channel_id=1, source_target_pairs={{0,8},{8,16},{16,24},{24,0},{1,9},{9,17},{17,25},{25,1},{2,10},{10... | collective-permute-start | bytes 491528 | tf_op jit(solution)/shard_map/ppermute | solution.py:529
  69.4 14.5 %collective-permute-start.29 = (bf16[160,512]{1,0:T(8,128)(2,1)S(1)}, bf16[160,512]{1,0:T(8,128)(2,1)S(1)}, u32[]{:S(2)}, u32[]{:S(2)}) collective-permute-start(bf16[160,512]{1,0:T(8,128)(2,1)S(1)} %get-tuple-element.51), channel_id=1, source_target_pairs={{0,16},{8,24},{16,0},{24,8},{1,17},{9,25},{17,1},{25,9},{2,18},{10... | collective-permute-start | bytes 491528 | tf_op jit(solution)/shard_map/ppermute | solution.py:529
  69.7 14.2 %collective-permute-start.30 = (bf16[160,512]{1,0:T(8,128)(2,1)S(1)}, bf16[160,512]{1,0:T(8,128)(2,1)S(1)}, u32[]{:S(2)}, u32[]{:S(2)}) collective-permute-start(bf16[160,512]{1,0:T(8,128)(2,1)S(1)} %get-tuple-element.52), channel_id=1, source_target_pairs={{0,24},{8,0},{16,8},{24,16},{1,25},{9,1},{17,9},{25,17},{2,26},{10... | collective-permute-start | bytes 491528 | tf_op jit(solution)/shard_map/ppermute | solution.py:529
  75.8 20.5 %collective-permute-start.25 = (bf16[128,1280]{1,0:T(8,128)(2,1)S(1)}, bf16[128,1280]{1,0:T(8,128)(2,1)S(1)}, u32[]{:S(2)}, u32[]{:S(2)}) collective-permute-start(bf16[128,1280]{1,0:T(8,128)(2,1)S(1)} %get-tuple-element.46), channel_id=1, source_target_pairs={{0,2},{2,0},{1,3},{3,1},{4,6},{6,4},{5,7},{7,5},{8,10},{10,8},{9,1... | collective-permute-start | bytes 983048 | tf_op jit(solution)/shard_map/ppermute | solution.py:529
  76.8 19.4 %collective-permute-start.26 = (bf16[128,1280]{1,0:T(8,128)(2,1)S(1)}, bf16[128,1280]{1,0:T(8,128)(2,1)S(1)}, u32[]{:S(2)}, u32[]{:S(2)}) collective-permute-start(bf16[128,1280]{1,0:T(8,128)(2,1)S(1)} %get-tuple-element.47), channel_id=1, source_target_pairs={{0,4},{4,0},{1,5},{5,1},{2,6},{6,2},{3,7},{7,3},{8,12},{12,8},{9,1... | collective-permute-start | bytes 983048 | tf_op jit(solution)/shard_map/ppermute | solution.py:529
  78.4 17.9 %collective-permute-start.27 = (bf16[128,1280]{1,0:T(8,128)(2,1)S(1)}, bf16[128,1280]{1,0:T(8,128)(2,1)S(1)}, u32[]{:S(2)}, u32[]{:S(2)}) collective-permute-start(bf16[128,1280]{1,0:T(8,128)(2,1)S(1)} %get-tuple-element.48), channel_id=1, source_target_pairs={{0,6},{2,4},{4,2},{6,0},{1,7},{3,5},{5,3},{7,1},{8,14},{10,12},{12... | collective-permute-start | bytes 983048 | tf_op jit(solution)/shard_map/ppermute | solution.py:647
  85.4 10.8 %collective-permute-start.31 = (bf16[160,512]{1,0:T(8,128)(2,1)S(1)}, bf16[160,512]{1,0:T(8,128)(2,1)S(1)}, u32[]{:S(2)}, u32[]{:S(2)}) collective-permute-start(bf16[160,512]{1,0:T(8,128)(2,1)S(1)} %get-tuple-element.53), channel_id=1, source_target_pairs={{0,2},{2,0},{1,3},{3,1},{4,6},{6,4},{5,7},{7,5},{8,10},{10,8},{9,1... | collective-permute-start | bytes 491528 | tf_op jit(solution)/shard_map/ppermute | solution.py:529
  86.4 11.7 %collective-permute-start.32 = (bf16[160,512]{1,0:T(8,128)(2,1)S(1)}, bf16[160,512]{1,0:T(8,128)(2,1)S(1)}, u32[]{:S(2)}, u32[]{:S(2)}) collective-permute-start(bf16[160,512]{1,0:T(8,128)(2,1)S(1)} %get-tuple-element.53), channel_id=1, source_target_pairs={{0,1},{1,0},{2,3},{3,2},{4,5},{5,4},{6,7},{7,6},{8,9},{9,8},{10,11... | collective-permute-start | bytes 491528 | tf_op jit(solution)/shard_map/ppermute | solution.py:529
  96.3 1.8 %collective-permute-start.33 = (bf16[160,512]{1,0:T(8,128)(2,1)S(1)}, bf16[160,512]{1,0:T(8,128)(2,1)}, u32[]{:S(2)}, u32[]{:S(2)}) collective-permute-start(bf16[160,512]{1,0:T(8,128)(2,1)S(1)} %collective-permute-done.31), channel_id=1, source_target_pairs={{0,1},{1,0},{2,3},{3,2},{4,5},{5,4},{6,7},{7,6},{8,9},{9,8},{10,11... | collective-permute-start | bytes 491528 | tf_op jit(solution)/shard_map/ppermute | solution.py:529
